TPU v7x, 32 devices: a whole 2x2x4 slice. The times are simulated.
32 devices in a mesh: row: 4 (over y, x), col: 8 (over z, core).
Axes of the slice: x: 2, y: 2, z: 4, core: 2. Of those that a mesh axis runs over, the one named last changes fastest.
Arguments:
- alignment: float32 [256, 256, 256], P('row', 'col'), may hold values from -6 to 6
- align_gain: float32 [256], replicated, may hold values from 0.5 to 1.5
- align_bias: float32 [256], replicated, may hold values from -1.75 to 1.75
- left_weight: float32 [256, 32], replicated, may hold values from -0.375 to 0.375
- right_weight: float32 [256, 32], replicated, may hold values from -0.375 to 0.375
- project_weight: float32 [1024, 128], replicated, may hold values from -3 to 3
- project_bias: float32 [128], replicated, may hold values from -1.75 to 1.75
- pair_state: float32 [256, 256, 128], P('row', 'col'), may hold values from -6 to 6
- pair_gain: float32 [128], replicated, may hold values from 0.5 to 1.5
- pair_bias: float32 [128], replicated, may hold values from -1.75 to 1.75
- hidden_weight: float32 [128, 512], replicated, may hold values from -0.5 to 0.5
- hidden_bias: float32 [512], replicated, may hold values from -1.75 to 1.75
- final_weight: float32 [512, 128], replicated, may hold values from -0.25 to 0.25
- final_bias: float32 [128], replicated, may hold values from -1.75 to 1.75
Outputs:
- pair_next: float32 [256, 256, 128], P('row', 'col')
All inputs are finite; a program needn't handle non-finite values.
Results may differ from a plain program's by a relative error of at most 0.0003.
Values sent between devices are 32-bit elements; how exact they have to be, the bound alone decides.
No kernel may reach another device: no remote copies, remote signals or barrier semaphores. Data moves between devices by JAX's collectives and lax.ppermute only.
A program may use at most 128 MiB of HBM per device.

v0:
```python
import functools

import jax
import jax.numpy as jnp
from jax import lax
from jax.experimental import pallas as pl
from jax.experimental.pallas import tpu as pltpu
from jax.sharding import PartitionSpec as P


LANES = 128
VMEM = 16 * 2**20
EPS = 1e-05
F32 = jnp.float32
BF16 = jnp.bfloat16


def split(values):
    high = values.astype(BF16)
    low = (values - high.astype(F32)).astype(BF16)
    return high, low


def dot(a, b):
    return jnp.dot(a, b, preferred_element_type=F32)


def norm(values, gain, offset):
    middle = jnp.mean(values, axis=-1, keepdims=True)
    centred = values - middle
    spread = jnp.mean(jnp.square(centred), axis=-1, keepdims=True)
    return centred * lax.rsqrt(spread + EPS) * gain + offset


def project_kernel(seqs, residues, width, chunks, x_hbm, gain_hbm, bias_hbm, lw_hbm, rw_hbm, *refs):
    left_refs, right_ref, place_ref = refs[:chunks], refs[chunks], refs[chunks + 1]
    x_ref, gain_ref, bias_ref, lw_ref, rw_ref, sems, w_high, w_low, y_ref, high_ref, low_ref = refs[chunks + 2 :]
    fold = lax.axis_size("col") // lax.axis_size("row")
    col = lax.axis_index("col")
    place_ref[0] = jnp.bitwise_xor(lax.div(col, fold), lax.axis_index("row")).astype(jnp.int32)
    place_ref[1] = lax.rem(col, fold).astype(jnp.int32)
    channels = x_ref.shape[1]
    per = LANES // width
    groups = residues // per
    block = seqs * residues
    steps = x_ref.shape[0] // block

    small = ((lw_hbm, lw_ref), (rw_hbm, rw_ref), (gain_hbm, gain_ref), (bias_hbm, bias_ref))
    copies = [pltpu.make_async_copy(a, b, sems.at[n]) for n, (a, b) in enumerate(small)]
    for step in range(steps):
        rows = pl.ds(step * block, block)
        copies.append(pltpu.make_async_copy(x_hbm.at[rows], x_ref.at[rows], sems.at[len(small) + step]))
    for copy in copies:
        copy.start()
    for copy in copies[: len(small)]:
        copy.wait()
    for at, ref in enumerate((lw_ref, rw_ref)):
        for e in range(per):
            zeros = [jnp.zeros((n * width, channels), F32) for n in (e, per - 1 - e)]
            placed = jnp.concatenate([z for z in (zeros[0], ref[...], zeros[1]) if z.shape[0]], axis=0)
            high, low = split(placed.T)
            w_high[e * channels : (e + 1) * channels, at * LANES : (at + 1) * LANES] = high
            w_low[e * channels : (e + 1) * channels, at * LANES : (at + 1) * LANES] = low

    for step in range(steps):
        copies[len(small) + step].wait()
        normed = norm(x_ref[step * block : (step + 1) * block, :], gain_ref[...], bias_ref[...])
        for part in range(channels // LANES):
            y_ref[step, part] = normed[:, part * LANES : (part + 1) * LANES]
        for e in range(per):
            for g in range(groups):
                for part in range(channels // LANES):
                    high, low = split(y_ref[step, part, pl.ds(g * per + e, seqs, stride=residues), :])
                    first = e * channels + part * LANES
                    high_ref[step, g * seqs : (g + 1) * seqs, first : first + LANES] = high
                    low_ref[step, g * seqs : (g + 1) * seqs, first : first + LANES] = low
        high, low = high_ref[step], low_ref[step]
        both = dot(high, w_high[...]) + dot(low, w_high[...]) + dot(high, w_low[...])
        share = groups // chunks
        for g in range(groups):
            rows = both[g * seqs : (g + 1) * seqs]
            to = slice(step * seqs, (step + 1) * seqs)
            at = g % share
            left_refs[g // share][to, at * LANES : (at + 1) * LANES] = rows[:, :LANES]
            right_ref[to, g * LANES : (g + 1) * LANES] = rows[:, LANES:]


def project(alignment, gain, bias, left_weight, right_weight, chunks):
    seq_local, residues, channels = alignment.shape
    width = left_weight.shape[1]
    steps = 4
    seqs = seq_local // steps
    per = LANES // width
    groups = residues // per
    span = residues * width
    outs = [jax.ShapeDtypeStruct((seq_local, span // chunks), F32)] * chunks + [
        jax.ShapeDtypeStruct((seq_local, span), F32),
        jax.ShapeDtypeStruct((2,), jnp.int32),
    ]
    return pl.pallas_call(
        functools.partial(project_kernel, seqs, residues, width, chunks),
        out_shape=outs,
        in_specs=[pl.BlockSpec(memory_space=pltpu.HBM)] * 5,
        out_specs=[pl.BlockSpec(memory_space=pltpu.VMEM)] * (len(outs) - 1) + [pl.BlockSpec(memory_space=pltpu.SMEM)],
        scratch_shapes=[
            pltpu.VMEM((seq_local * residues, channels), F32),
            pltpu.VMEM((1, channels), F32),
            pltpu.VMEM((1, channels), F32),
            pltpu.VMEM((width, channels), F32),
            pltpu.VMEM((width, channels), F32),
            pltpu.SemaphoreType.DMA((4 + steps,)),
            pltpu.VMEM((per * channels, 2 * LANES), BF16),
            pltpu.VMEM((per * channels, 2 * LANES), BF16),
            pltpu.VMEM((steps, channels // LANES, seqs * residues, LANES), F32),
            pltpu.VMEM((steps, groups * seqs, per * channels), BF16),
            pltpu.VMEM((steps, groups * seqs, per * channels), BF16),
        ],
        cost_estimate=pl.CostEstimate(flops=6 * 10**9, bytes_accessed=4 * 10**6, transcendentals=0),
        compiler_params=pltpu.CompilerParams(vmem_limit_bytes=VMEM),
        name="project",
    )(
        *(
            pltpu.with_memory_space_constraint(a, pltpu.HBM)
            for a in (
                alignment.reshape(seq_local * residues, channels),
                gain.reshape(1, channels),
                bias.reshape(1, channels),
                left_weight.T,
                right_weight.T,
            )
        )
    )


def weights_kernel(width, wp_ref, wh_ref, wf_ref, wp_out, wh_out, wf_out):
    pair = wp_ref.shape[1]
    for d in range(width):
        high, low = split(wp_ref[pl.ds(d, width, stride=width), :])
        wp_out[d * width : (d + 1) * width, :pair] = high
        wp_out[d * width : (d + 1) * width, pair:] = low
    high, low = split(wh_ref[...])
    wh_out[:pair] = high
    wh_out[pair : 2 * pair] = high
    wh_out[2 * pair :] = low
    high, low = split(wf_ref[...])
    wf_out[:, :pair] = high
    wf_out[:, pair:] = low


def prepare_weights(project_weight, hidden_weight, final_weight, width):
    pair, hidden = hidden_weight.shape
    return pl.pallas_call(
        functools.partial(weights_kernel, width),
        out_shape=[
            jax.ShapeDtypeStruct((width * width, 2 * pair), BF16),
            jax.ShapeDtypeStruct((3 * pair, hidden), BF16),
            jax.ShapeDtypeStruct((hidden, 2 * pair), BF16),
        ],
        cost_estimate=pl.CostEstimate(flops=10**9, bytes_accessed=2 * 10**6, transcendentals=0),
        compiler_params=pltpu.CompilerParams(vmem_limit_bytes=VMEM),
        name="weights",
    )(project_weight, hidden_weight, final_weight)


def turn_kernel(residues, width, scale, *refs):
    parts, out_ref, turned = refs[:-2], refs[-2], refs[-1]
    seqs = parts[0].shape[0]
    total = seqs * len(parts)
    whole = jnp.concatenate([p[...] for p in parts], axis=0) * scale
    for part in range(total // LANES):
        turned[part] = whole[part * LANES : (part + 1) * LANES].T
    for d in range(width):
        rows = slice(d * residues, (d + 1) * residues)
        for part in range(total // LANES):
            high, low = split(turned[part, pl.ds(d, residues, stride=width), :])
            for at, value in ((0, high), (total, low), (2 * total, high)):
                first = at + part * LANES
                out_ref[rows, first : first + LANES] = value


def turn(parts, residues, width):
    seqs, span = parts[0].shape
    total = seqs * len(parts)
    return pl.pallas_call(
        functools.partial(turn_kernel, residues, width, 1.0 / total),
        out_shape=jax.ShapeDtypeStruct((span, 3 * total), BF16),
        scratch_shapes=[pltpu.VMEM((total // LANES, span, LANES), F32)],
        cost_estimate=pl.CostEstimate(flops=2 * 10**9, bytes_accessed=3 * 10**6, transcendentals=0),
        compiler_params=pltpu.CompilerParams(vmem_limit_bytes=VMEM),
        name="turn",
    )(*parts)


def route_kernel(slots, t_ref, *refs):
    ins, outs = refs[:-slots], refs[-slots:]
    for t in range(slots):

        @pl.when(t_ref[0] == t)
        def _():
            for m in range(slots):
                at = m ^ t
                value = ins[at][...]
                if at == slots - 1:
                    for extra in ins[slots:]:
                        value = value + extra[...]
                outs[m][...] = value


def route(t, slots, ins):
    spec = pl.BlockSpec(memory_space=pltpu.VMEM)
    return pl.pallas_call(
        functools.partial(route_kernel, slots),
        out_shape=[jax.ShapeDtypeStruct(ins[0].shape, F32)] * slots,
        in_specs=[pl.BlockSpec(memory_space=pltpu.SMEM)] + [spec] * len(ins),
        out_specs=[spec] * slots,
        cost_estimate=pl.CostEstimate(flops=10**6, bytes_accessed=2 * 10**6, transcendentals=0),
        compiler_params=pltpu.CompilerParams(vmem_limit_bytes=VMEM),
        name="route",
    )(t, *ins)


def pack_kernel(*refs):
    rows = refs[0].shape[0]
    for n, ref in enumerate(refs[:-1]):
        refs[-1][n * rows : (n + 1) * rows, :] = ref[...]


def pack(parts):
    rows, span = parts[0].shape
    return pl.pallas_call(
        pack_kernel,
        out_shape=jax.ShapeDtypeStruct((rows * len(parts), span), F32),
        cost_estimate=pl.CostEstimate(flops=10**6, bytes_accessed=10**6, transcendentals=0),
        compiler_params=pltpu.CompilerParams(vmem_limit_bytes=VMEM),
        name="pack",
    )(*parts)


def pair_kernel(parts, steps, tile, width, at_ref, *refs):
    l_refs = refs[:parts]
    rt_ref, wp_ref, wh_ref, wf_ref, pb_ref, pg_ref, po_ref, hb_ref, fb_ref, ps_ref = refs[parts : parts + 10]
    out_ref, high_ref, low_ref = refs[-3:]
    residues, pair = ps_ref.shape[1:]
    per = LANES // width
    left = l_refs[0][...]
    for n in range(1, parts):
        left = jnp.where(pl.program_id(0) >= n * steps, l_refs[n][...], left)
    high, low = split(left)
    left = jnp.concatenate([high, high, low], axis=0)
    lane = lax.broadcasted_iota(jnp.int32, (residues, LANES), 1) // width
    odd, upper = lane % 2 == 1, lane >= 2
    block = 2 * per
    for first in range(0, width, block):
        outer = dot(rt_ref[first * residues : (first + block) * residues, :], left)
        for d0 in range(0, block, per):
            for g in range(tile // per):
                u = []
                for d in range(per):
                    rows = (d0 + d) * residues
                    v = outer[rows : rows + residues, g * LANES : (g + 1) * LANES]
                    u.append(pltpu.roll(v, d * width, 1) if d else v)
                x = [jnp.where(odd, u[(n + 1) % per], u[n]) for n in range(per)]
                for i in range(per):
                    n = -i % per
                    y = jnp.where(upper, x[(n + 2) % per], x[n])
                    y = pltpu.roll(y, (per - i) * width, 1) if i else y
                    high, low = split(y)
                    rows = slice((g * per + i) * residues, (g * per + i + 1) * residues)
                    lanes = slice((first + d0) * width, (first + d0 + per) * width)
                    high_ref[rows, lanes] = high
                    low_ref[rows, lanes] = low
    both = dot(high_ref[...], wp_ref[...])
    update = both[:, :pair] + both[:, pair:] + dot(low_ref[...], wp_ref[:, :pair])
    updated = ps_ref[...].reshape(tile * residues, pair) + update + pb_ref[...]
    high, low = split(norm(updated, pg_ref[...], po_ref[...]))
    hidden = jnp.maximum(dot(jnp.concatenate([high, low, high], axis=1), wh_ref[...]) + hb_ref[...], 0.0)
    high, low = split(hidden)
    both = dot(high, wf_ref[...])
    output = both[:, :pair] + both[:, pair:] + dot(low, wf_ref[:, :pair]) + fb_ref[...]
    out_ref[...] = (updated + output).reshape(tile, residues, pair)


def pair_update(place, members, chunk, lefts, rt, weights, vectors, pair_state, out, width):
    tile = 8
    wp, wh, wf = weights
    seqs, span = lefts[0].shape
    steps = span // (tile * width)
    residues, pair = pair_state.shape[1:]
    whole = lambda a: pl.BlockSpec(a.shape, lambda s, at: (0,) * a.ndim, pipeline_mode=pl.Buffered(1))
    tiles = residues // tile

    def tile_at(s, place):
        member = jnp.bitwise_xor(place[1], members[0])
        for n in range(1, len(members)):
            member = jnp.where(s >= n * steps, jnp.bitwise_xor(place[1], members[n]), member)
        return member * tiles + chunk * steps + lax.rem(s, steps), 0, 0

    rows = pl.BlockSpec((tile, residues, pair), tile_at)
    fixed = [pltpu.with_memory_space_constraint(a, pltpu.VMEM) for a in (rt, wp, wh, wf)]
    operands = [*lefts, *fixed, *vectors, pair_state]
    specs = [
        pl.BlockSpec((seqs, tile * width), lambda s, at, n=n: (0, jnp.clip(s - n * steps, 0, steps - 1)))
        for n in range(len(lefts))
    ]
    specs += [whole(a) for a in operands[len(lefts) : -1]] + [rows]
    aliases = {}
    if out is not None:
        aliases = {len(operands) + 1: 0}
        operands.append(out)
        specs.append(pl.BlockSpec(memory_space=pl.ANY))
    return pl.pallas_call(
        functools.partial(pair_kernel, len(lefts), steps, tile, width),
        out_shape=jax.ShapeDtypeStruct(pair_state.shape, F32),
        grid_spec=pltpu.PrefetchScalarGridSpec(
            num_scalar_prefetch=1,
            grid=(steps * len(lefts),),
            in_specs=specs,
            out_specs=rows,
            scratch_shapes=[
                pltpu.VMEM((tile * residues, width * width), BF16),
                pltpu.VMEM((tile * residues, width * width), BF16),
            ],
        ),
        input_output_aliases=aliases,
        cost_estimate=pl.CostEstimate(flops=steps * len(lefts) * 10**9, bytes_accessed=4 * 10**6, transcendentals=0),
        compiler_params=pltpu.CompilerParams(vmem_limit_bytes=VMEM),
        name="pair",
    )(place, *operands)


def on_device(
    alignment,
    align_gain,
    align_bias,
    left_weight,
    right_weight,
    project_weight,
    project_bias,
    pair_state,
    pair_gain,
    pair_bias,
    hidden_weight,
    hidden_bias,
    final_weight,
    final_bias,
):
    chunks = 2
    residues = alignment.shape[1]
    width = left_weight.shape[1]
    rows = lax.axis_size("row")
    cols = lax.axis_size("col")
    fold = cols // rows

    def along_groups(value, pairs):
        return lax.ppermute(value, "col", [(a * fold + k, b * fold + k) for a, b in pairs for k in range(fold)])

    def along_rows(value, m):
        return lax.ppermute(value, "row", [(a, a ^ m) for a in range(rows)])

    def along_members(value, n):
        return lax.ppermute(value, "col", [(a, a ^ n) for a in range(cols)])

    *lefts, right, place = project(alignment, align_gain, align_bias, left_weight, right_weight, chunks)

    def spread(left):
        if rows != 4:
            return [left] + [along_groups(left, [(a, a ^ m) for a in range(rows)]) for m in range(1, rows)]
        two = along_groups(left, [(a, a ^ 2) for a in range(4)])
        one = along_groups(left, [(a, a ^ 1) for a in range(4)])
        three = along_groups(left, [(1, 2), (2, 1)])
        relayed = along_groups(two, [(1, 0), (2, 3)])
        return [left, one, two, three, relayed]

    slots = [spread(left) for left in lefts]
    rights = [right] + [along_rows(right, m) for m in range(1, rows)]
    weights = prepare_weights(project_weight, hidden_weight, final_weight, width)
    rt = turn(rights, residues, width)
    vectors = [v.reshape(1, -1) for v in (project_bias, pair_gain, pair_bias, hidden_bias, final_bias)]

    out = None
    for chunk in range(chunks):
        routed = route(place, rows, slots[chunk])
        mine = [routed[0]] + [along_rows(routed[m], m) for m in range(1, rows)]
        packed = pack(mine)
        blocks = [packed] + [along_members(packed, n) for n in range(1, fold)]
        calls = [[n] for n in range(fold)] if chunk == chunks - 1 else [list(range(fold))]
        for members in calls:
            out = pair_update(
                place, members, chunk, [blocks[n] for n in members], rt, weights, vectors, pair_state, out, width
            )
    return out


def solution(mesh):
    placed = (
        P("row", "col", None),
        P(),
        P(),
        P(),
        P(),
        P(),
        P(),
        P("row", "col", None),
        P(),
        P(),
        P(),
        P(),
        P(),
        P(),
    )

    return jax.shard_map(on_device, mesh=mesh, in_specs=placed, out_specs=P("row", "col", None), check_vma=False)
```

profile of v0, /device:TPU:0, one launch (start us, length us, event | category | flops | bytes accessed | tf_op | source)
XLA Modules:
  0.0 73.6 jit_solution(13534117682214140449)
XLA Ops:
  0.0 0.0 copy-start.1
  0.0 0.0 copy-start.2
  0.0 0.0 copy-start.3
  0.0 5.5 %project.1 = (f32[64,512]{1,0:T(8,128)S(1)}, f32[64,512]{1,0:T(8,128)S(1)}, f32[64,1024]{1,0:T(8,128)S(1)}, s32[2]{0:T(128)S(1)}) custom-call(f32[2048,256]{1,0:T(8,128)} %bitcast.25, f32[1,256]{1,0:T(1,128)} %bitcast.28, f32[1,256]{1,0:T(1,128)} %bitcast.29, f32[32,256]{1,0:T(8,128)} %bitcast.26, f32[32,256]{1,0:T(8,128)} %bitcast.27), custom_call_target="tpu_custom_call" | custom-call | flops 6000000000 | bytes 4000000 | tf_op jit(solution)/shard_map/project/pallas_call | solution.py:100
  5.5 4.1 %collective-permute-start.12 = (f32[64,512]{1,0:T(8,128)S(1)}, f32[64,512]{1,0:T(8,128)S(1)}, u32[]{:S(2)}, u32[]{:S(2)}) collective-permute-start(f32[64,512]{1,0:T(8,128)S(1)} %get-tuple-element.30.refs_0_), channel_id=1, source_target_pairs={{0,4},{1,5},{2,6},{3,7},{4,0},{5,1},{6,2},{7,3},{8,12},{9,13},{10,... | collective-permute-start | bytes 393224 | tf_op jit(solution)/shard_map/ppermute | solution.py:355
  9.6 1.6 %collective-permute-start.11 = (f32[64,512]{1,0:T(8,128)S(1)}, f32[64,512]{1,0:T(8,128)S(1)}, u32[]{:S(2)}, u32[]{:S(2)}) collective-permute-start(f32[64,512]{1,0:T(8,128)S(1)} %get-tuple-element.30.refs_0_), channel_id=1, source_target_pairs={{0,2},{1,3},{2,0},{3,1},{4,6},{5,7},{6,4},{7,5},{8,10},{9,11},{10,... | collective-permute-start | bytes 393224 | tf_op jit(solution)/shard_map/ppermute | solution.py:355
  11.2 0.7 collective-permute-start.13
  11.8 4.9 %collective-permute-done.12.refs_2_ = f32[64,512]{1,0:T(8,128)S(1)} collective-permute-done((f32[64,512]{1,0:T(8,128)S(1)}, f32[64,512]{1,0:T(8,128)S(1)}, u32[]{:S(2)}, u32[]{:S(2)}) %collective-permute-start.12) | collective-permute-done | bytes 131104 | tf_op jit(solution)/shard_map/ppermute | solution.py:355
  16.8 1.3 %collective-permute-start.14 = (f32[64,512]{1,0:T(8,128)S(1)}, f32[64,512]{1,0:T(8,128)S(1)}, u32[]{:S(2)}, u32[]{:S(2)}) collective-permute-start(f32[64,512]{1,0:T(8,128)S(1)} %collective-permute-done.12.refs_2_), channel_id=1, source_target_pairs={{2,0},{3,1},{4,6},{5,7},{10,8},{11,9},{12,14},{13,15},{18,16},{19,... | collective-permute-start | bytes 393224 | tf_op jit(solution)/shard_map/ppermute | solution.py:355
  18.0 0.0 collective-permute-done.11.refs_1_
  18.1 0.0 collective-permute-done.13.refs_3_
  18.1 5.5 %collective-permute-done.14.refs_4_ = f32[64,512]{1,0:T(8,128)S(1)} collective-permute-done((f32[64,512]{1,0:T(8,128)S(1)}, f32[64,512]{1,0:T(8,128)S(1)}, u32[]{:S(2)}, u32[]{:S(2)}) %collective-permute-start.14) | collective-permute-done | bytes 131104 | tf_op jit(solution)/shard_map/ppermute | solution.py:355
  23.6 0.6 route.3
  24.2 1.7 %collective-permute-start.15 = (f32[64,512]{1,0:T(8,128)S(1)}, f32[64,512]{1,0:T(8,128)S(1)}, u32[]{:S(2)}, u32[]{:S(2)}) collective-permute-start(f32[64,512]{1,0:T(8,128)S(1)} %get-tuple-element.32), channel_id=1, source_target_pairs={{0,8},{8,0},{16,24},{24,16},{1,9},{9,1},{17,25},{25,17},{2,10},{10... | collective-permute-start | bytes 393224 | tf_op jit(solution)/shard_map/ppermute | solution.py:358
  25.9 1.5 %collective-permute-start.16 = (f32[64,512]{1,0:T(8,128)S(1)}, f32[64,512]{1,0:T(8,128)S(1)}, u32[]{:S(2)}, u32[]{:S(2)}) collective-permute-start(f32[64,512]{1,0:T(8,128)S(1)} %get-tuple-element.33), channel_id=1, source_target_pairs={{0,16},{8,24},{16,0},{24,8},{1,17},{9,25},{17,1},{25,9},{2,18},{10... | collective-permute-start | bytes 393224 | tf_op jit(solution)/shard_map/ppermute | solution.py:358
  27.4 0.4 collective-permute-start.17
  27.8 1.2 %collective-permute-start.1 = (f32[64,512]{1,0:T(8,128)S(1)}, f32[64,512]{1,0:T(8,128)S(1)}, u32[]{:S(2)}, u32[]{:S(2)}) collective-permute-start(f32[64,512]{1,0:T(8,128)S(1)} %get-tuple-element.21.refs_0_), channel_id=1, source_target_pairs={{0,4},{1,5},{2,6},{3,7},{4,0},{5,1},{6,2},{7,3},{8,12},{9,13},{10,... | collective-permute-start | bytes 393224 | tf_op jit(solution)/shard_map/ppermute | solution.py:355
  29.0 2.5 %collective-permute-start = (f32[64,512]{1,0:T(8,128)S(1)}, f32[64,512]{1,0:T(8,128)S(1)}, u32[]{:S(2)}, u32[]{:S(2)}) collective-permute-start(f32[64,512]{1,0:T(8,128)S(1)} %get-tuple-element.21.refs_0_), channel_id=1, source_target_pairs={{0,2},{1,3},{2,0},{3,1},{4,6},{5,7},{6,4},{7,5},{8,10},{9,11},{10,... | collective-permute-start | bytes 393224 | tf_op jit(solution)/shard_map/ppermute | solution.py:355
  31.5 0.0 collective-permute-done.15.refs_1_
  31.5 0.0 collective-permute-done.16.refs_2_
  31.5 1.8 %collective-permute-done.17.refs_3_ = f32[64,512]{1,0:T(8,128)S(1)} collective-permute-done((f32[64,512]{1,0:T(8,128)S(1)}, f32[64,512]{1,0:T(8,128)S(1)}, u32[]{:S(2)}, u32[]{:S(2)}) %collective-permute-start.17) | collective-permute-done | bytes 131104 | tf_op jit(solution)/shard_map/ppermute | solution.py:358
  33.3 0.1 collective-permute-start.18
  33.4 0.7 collective-permute-start.2
  34.1 0.7 %collective-permute-start.10 = (f32[64,1024]{1,0:T(8,128)S(1)}, f32[64,1024]{1,0:T(8,128)S(1)}, u32[]{:S(2)}, u32[]{:S(2)}) collective-permute-start(f32[64,1024]{1,0:T(8,128)S(1)} %get-tuple-element.26.refs_0_), channel_id=1, source_target_pairs={{0,24},{8,16},{16,8},{24,0},{1,25},{9,17},{17,9},{25,1},{2,26},{10... | collective-permute-start | bytes 786440 | tf_op jit(solution)/shard_map/ppermute | solution.py:358
  34.8 0.3 collective-permute-done.1.refs_2_
  35.2 1.6 %collective-permute-start.8 = (f32[64,1024]{1,0:T(8,128)S(1)}, f32[64,1024]{1,0:T(8,128)S(1)}, u32[]{:S(2)}, u32[]{:S(2)}) collective-permute-start(f32[64,1024]{1,0:T(8,128)S(1)} %get-tuple-element.26.refs_0_), channel_id=1, source_target_pairs={{0,8},{8,0},{16,24},{24,16},{1,9},{9,1},{17,25},{25,17},{2,10},{10... | collective-permute-start | bytes 786440 | tf_op jit(solution)/shard_map/ppermute | solution.py:358
  36.7 0.0 collective-permute-done.refs_1_
  36.7 1.5 %collective-permute-start.9 = (f32[64,1024]{1,0:T(8,128)S(1)}, f32[64,1024]{1,0:T(8,128)S(1)}, u32[]{:S(2)}, u32[]{:S(2)}) collective-permute-start(f32[64,1024]{1,0:T(8,128)S(1)} %get-tuple-element.26.refs_0_), channel_id=1, source_target_pairs={{0,16},{8,24},{16,0},{24,8},{1,17},{9,25},{17,1},{25,9},{2,18},{10... | collective-permute-start | bytes 786440 | tf_op jit(solution)/shard_map/ppermute | solution.py:358
  38.3 0.0 collective-permute-done.2.refs_3_
  38.3 1.3 %collective-permute-start.3 = (f32[64,512]{1,0:T(8,128)S(1)}, f32[64,512]{1,0:T(8,128)S(1)}, u32[]{:S(2)}, u32[]{:S(2)}) collective-permute-start(f32[64,512]{1,0:T(8,128)S(1)} %collective-permute-done.1.refs_2_), channel_id=1, source_target_pairs={{2,0},{3,1},{4,6},{5,7},{10,8},{11,9},{12,14},{13,15},{18,16},{19,... | collective-permute-start | bytes 393224 | tf_op jit(solution)/shard_map/ppermute | solution.py:355
  39.6 0.0 copy-done.1
  39.6 0.0 copy-done.2
  39.6 0.0 copy-done.3
  39.6 0.4 weights.1
  40.0 6.3 %collective-permute-done.3.refs_4_ = f32[64,512]{1,0:T(8,128)S(1)} collective-permute-done((f32[64,512]{1,0:T(8,128)S(1)}, f32[64,512]{1,0:T(8,128)S(1)}, u32[]{:S(2)}, u32[]{:S(2)}) %collective-permute-start.3) | collective-permute-done | bytes 131104 | tf_op jit(solution)/shard_map/ppermute | solution.py:355
  46.3 0.6 route.2
  46.9 0.6 collective-permute-start.4
  47.5 0.0 collective-permute-done.10.refs_3_
  47.5 0.8 %collective-permute-start.5 = (f32[64,512]{1,0:T(8,128)S(1)}, f32[64,512]{1,0:T(8,128)S(1)}, u32[]{:S(2)}, u32[]{:S(2)}) collective-permute-start(f32[64,512]{1,0:T(8,128)S(1)} %get-tuple-element.24), channel_id=1, source_target_pairs={{0,16},{8,24},{16,0},{24,8},{1,17},{9,25},{17,1},{25,9},{2,18},{10... | collective-permute-start | bytes 393224 | tf_op jit(solution)/shard_map/ppermute | solution.py:358
  48.3 0.1 collective-permute-done.8.refs_1_
  48.4 0.0 copy-start
  48.4 0.0 copy-start.4
  48.4 0.0 copy-start.5
  48.4 0.0 copy-start.6
  48.4 0.0 copy-start.7
  48.5 0.0 copy-start.8
  48.5 2.1 %collective-permute-start.6 = (f32[64,512]{1,0:T(8,128)S(1)}, f32[64,512]{1,0:T(8,128)S(1)}, u32[]{:S(2)}, u32[]{:S(2)}) collective-permute-start(f32[64,512]{1,0:T(8,128)S(1)} %get-tuple-element.25), channel_id=1, source_target_pairs={{0,24},{8,16},{16,8},{24,0},{1,25},{9,17},{17,9},{25,1},{2,26},{10... | collective-permute-start | bytes 393224 | tf_op jit(solution)/shard_map/ppermute | solution.py:358
  50.6 0.0 collective-permute-done.9.refs_2_
  50.6 0.9 %turn.1.refs_2_.refs_1_ = bf16[1024,768]{1,0:T(8,128)(2,1)S(1)} custom-call(f32[64,1024]{1,0:T(8,128)S(1)} %get-tuple-element.26.refs_0_, f32[64,1024]{1,0:T(8,128)S(1)} %collective-permute-done.8.refs_1_, f32[64,1024]{1,0:T(8,128)S(1)} %collective-permute-done.9.refs_2_, f32[64,1024]{1,0:T(8,128)S(1)} %collective-permute-done.10.refs_3_), custom_call_target="tpu_custom_call" | custom-call | flops 2000000000 | bytes 3000000 | tf_op jit(solution)/shard_map/turn/pallas_call | solution.py:184
  51.6 0.7 collective-permute-done.4.refs_1_
  52.2 1.0 %collective-permute-done.5.refs_2_ = f32[64,512]{1,0:T(8,128)S(1)} collective-permute-done((f32[64,512]{1,0:T(8,128)S(1)}, f32[64,512]{1,0:T(8,128)S(1)}, u32[]{:S(2)}, u32[]{:S(2)}) %collective-permute-start.5) | collective-permute-done | bytes 131104 | tf_op jit(solution)/shard_map/ppermute | solution.py:358
  53.3 2.0 %collective-permute-done.6.refs_3_ = f32[64,512]{1,0:T(8,128)S(1)} collective-permute-done((f32[64,512]{1,0:T(8,128)S(1)}, f32[64,512]{1,0:T(8,128)S(1)}, u32[]{:S(2)}, u32[]{:S(2)}) %collective-permute-start.6) | collective-permute-done | bytes 131104 | tf_op jit(solution)/shard_map/ppermute | solution.py:358
  55.3 0.1 collective-permute-start.7
  55.4 0.0 collective-permute-done.18.refs_1_
  55.4 0.0 copy-done
  55.4 0.0 copy-done.4
  55.4 0.0 copy-done.5
  55.5 0.0 copy-done.6
  55.5 0.0 copy-done.7
  55.5 0.0 copy-done.8
  55.5 8.5 %pair.3.refs_11_ = f32[64,32,128]{2,1,0:T(8,128)} custom-call(s32[2]{0:T(128)S(1)} %get-tuple-element.20.t_ref.at_ref, f32[256,512]{1,0:T(8,128)S(1)} %pack.3.refs_0_, f32[256,512]{1,0:T(8,128)S(1)} %collective-permute-done.18.refs_1_, bf16[1024,768]{1,0:T(8,128)(2,1)S(1)} %turn.1.refs_2_.refs_1_, bf16[1024,256]{1,0:T(8,128)(2,1)S(1)} %get-tuple-element.27.refs_3_.refs_2_, ...), custom_call_target="tpu_custom_call" | custom-call | flops 4000000000 | bytes 4000000 | tf_op jit(solution)/shard_map/pair/pallas_call | solution.py:311
  64.0 4.8 %pair.4.refs_11_ = f32[64,32,128]{2,1,0:T(8,128)} custom-call(s32[2]{0:T(128)S(1)} %get-tuple-element.20.t_ref.at_ref, f32[256,512]{1,0:T(8,128)S(1)} %pack.2.refs_0_, bf16[1024,768]{1,0:T(8,128)(2,1)S(1)} %turn.1.refs_2_.refs_1_, bf16[1024,256]{1,0:T(8,128)(2,1)S(1)} %get-tuple-element.27.refs_3_.refs_2_, ...), custom_call_target="tpu_custom_call", output_to_operand_aliasing={{}: (12, {})} | custom-call | flops 2000000000 | bytes 4000000 | tf_op jit(solution)/shard_map/pair/pallas_call | solution.py:311
  68.8 0.0 collective-permute-done.7.refs_0_
  68.8 4.8 %pair.5 = f32[64,32,128]{2,1,0:T(8,128)} custom-call(s32[2]{0:T(128)S(1)} %get-tuple-element.20.t_ref.at_ref, f32[256,512]{1,0:T(8,128)S(1)} %collective-permute-done.7.refs_0_, bf16[1024,768]{1,0:T(8,128)(2,1)S(1)} %turn.1.refs_2_.refs_1_, bf16[1024,256]{1,0:T(8,128)(2,1)S(1)} %get-tuple-element.27.refs_3_.refs_2_, ...), custom_call_target="tpu_custom_call", output_to_operand_aliasing={{}: (12, {})} | custom-call | flops 2000000000 | bytes 4000000 | tf_op jit(solution)/shard_map/pair/pallas_call | solution.py:311
  (2 shorter events, 0.1 us)
Async XLA Ops:
  0.0 39.6 %copy-start.1 = (f32[1024,128]{1,0:T(8,128)S(1)}, f32[1024,128]{1,0:T(8,128)}, u32[]{:S(2)}) copy-start(f32[1024,128]{1,0:T(8,128)} %wp_ref.1) | copy-start | bytes 1572868
  0.0 39.6 %copy-start.2 = (f32[128,512]{1,0:T(8,128)S(1)}, f32[128,512]{1,0:T(8,128)}, u32[]{:S(2)}) copy-start(f32[128,512]{1,0:T(8,128)} %wh_ref.1) | copy-start | bytes 786436
  0.0 39.6 %copy-start.3 = (f32[512,128]{1,0:T(8,128)S(1)}, f32[512,128]{1,0:T(8,128)}, u32[]{:S(2)}) copy-start(f32[512,128]{1,0:T(8,128)} %wf_ref.1) | copy-start | bytes 786436
  5.5 11.3 %collective-permute-start.12 = (f32[64,512]{1,0:T(8,128)S(1)}, f32[64,512]{1,0:T(8,128)S(1)}, u32[]{:S(2)}, u32[]{:S(2)}) collective-permute-start(f32[64,512]{1,0:T(8,128)S(1)} %get-tuple-element.30.refs_0_), channel_id=1, source_target_pairs={{0,4},{1,5},{2,6},{3,7},{4,0},{5,1},{6,2},{7,3},{8,12},{9,13},{10,... | collective-permute-start | bytes 393224 | tf_op jit(solution)/shard_map/ppermute | solution.py:355
  9.6 8.4 %collective-permute-start.11 = (f32[64,512]{1,0:T(8,128)S(1)}, f32[64,512]{1,0:T(8,128)S(1)}, u32[]{:S(2)}, u32[]{:S(2)}) collective-permute-start(f32[64,512]{1,0:T(8,128)S(1)} %get-tuple-element.30.refs_0_), channel_id=1, source_target_pairs={{0,2},{1,3},{2,0},{3,1},{4,6},{5,7},{6,4},{7,5},{8,10},{9,11},{10,... | collective-permute-start | bytes 393224 | tf_op jit(solution)/shard_map/ppermute | solution.py:355
  11.2 6.9 %collective-permute-start.13 = (f32[64,512]{1,0:T(8,128)S(1)}, f32[64,512]{1,0:T(8,128)S(1)}, u32[]{:S(2)}, u32[]{:S(2)}) collective-permute-start(f32[64,512]{1,0:T(8,128)S(1)} %get-tuple-element.30.refs_0_), channel_id=1, source_target_pairs={{2,4},{3,5},{4,2},{5,3},{10,12},{11,13},{12,10},{13,11},{18,20},{1... | collective-permute-start | bytes 393224 | tf_op jit(solution)/shard_map/ppermute | solution.py:355
  16.8 6.8 %collective-permute-start.14 = (f32[64,512]{1,0:T(8,128)S(1)}, f32[64,512]{1,0:T(8,128)S(1)}, u32[]{:S(2)}, u32[]{:S(2)}) collective-permute-start(f32[64,512]{1,0:T(8,128)S(1)} %collective-permute-done.12.refs_2_), channel_id=1, source_target_pairs={{2,0},{3,1},{4,6},{5,7},{10,8},{11,9},{12,14},{13,15},{18,16},{19,... | collective-permute-start | bytes 393224 | tf_op jit(solution)/shard_map/ppermute | solution.py:355
  24.2 7.3 %collective-permute-start.15 = (f32[64,512]{1,0:T(8,128)S(1)}, f32[64,512]{1,0:T(8,128)S(1)}, u32[]{:S(2)}, u32[]{:S(2)}) collective-permute-start(f32[64,512]{1,0:T(8,128)S(1)} %get-tuple-element.32), channel_id=1, source_target_pairs={{0,8},{8,0},{16,24},{24,16},{1,9},{9,1},{17,25},{25,17},{2,10},{10... | collective-permute-start | bytes 393224 | tf_op jit(solution)/shard_map/ppermute | solution.py:358
  25.9 5.6 %collective-permute-start.16 = (f32[64,512]{1,0:T(8,128)S(1)}, f32[64,512]{1,0:T(8,128)S(1)}, u32[]{:S(2)}, u32[]{:S(2)}) collective-permute-start(f32[64,512]{1,0:T(8,128)S(1)} %get-tuple-element.33), channel_id=1, source_target_pairs={{0,16},{8,24},{16,0},{24,8},{1,17},{9,25},{17,1},{25,9},{2,18},{10... | collective-permute-start | bytes 393224 | tf_op jit(solution)/shard_map/ppermute | solution.py:358
  27.4 5.9 %collective-permute-start.17 = (f32[64,512]{1,0:T(8,128)S(1)}, f32[64,512]{1,0:T(8,128)S(1)}, u32[]{:S(2)}, u32[]{:S(2)}) collective-permute-start(f32[64,512]{1,0:T(8,128)S(1)} %get-tuple-element.34), channel_id=1, source_target_pairs={{0,24},{8,16},{16,8},{24,0},{1,25},{9,17},{17,9},{25,1},{2,26},{10... | collective-permute-start | bytes 393224 | tf_op jit(solution)/shard_map/ppermute | solution.py:358
  27.8 7.4 %collective-permute-start.1 = (f32[64,512]{1,0:T(8,128)S(1)}, f32[64,512]{1,0:T(8,128)S(1)}, u32[]{:S(2)}, u32[]{:S(2)}) collective-permute-start(f32[64,512]{1,0:T(8,128)S(1)} %get-tuple-element.21.refs_0_), channel_id=1, source_target_pairs={{0,4},{1,5},{2,6},{3,7},{4,0},{5,1},{6,2},{7,3},{8,12},{9,13},{10,... | collective-permute-start | bytes 393224 | tf_op jit(solution)/shard_map/ppermute | solution.py:355
  29.0 7.7 %collective-permute-start = (f32[64,512]{1,0:T(8,128)S(1)}, f32[64,512]{1,0:T(8,128)S(1)}, u32[]{:S(2)}, u32[]{:S(2)}) collective-permute-start(f32[64,512]{1,0:T(8,128)S(1)} %get-tuple-element.21.refs_0_), channel_id=1, source_target_pairs={{0,2},{1,3},{2,0},{3,1},{4,6},{5,7},{6,4},{7,5},{8,10},{9,11},{10,... | collective-permute-start | bytes 393224 | tf_op jit(solution)/shard_map/ppermute | solution.py:355
  33.3 22.1 %collective-permute-start.18 = (f32[256,512]{1,0:T(8,128)S(1)}, f32[256,512]{1,0:T(8,128)S(1)}, u32[]{:S(2)}, u32[]{:S(2)}) collective-permute-start(f32[256,512]{1,0:T(8,128)S(1)} %pack.3.refs_0_), channel_id=1, source_target_pairs={{0,1},{1,0},{2,3},{3,2},{4,5},{5,4},{6,7},{7,6},{8,9},{9,8},{10,11... | collective-permute-start | bytes 1572872 | tf_op jit(solution)/shard_map/ppermute | solution.py:361
  33.4 4.9 %collective-permute-start.2 = (f32[64,512]{1,0:T(8,128)S(1)}, f32[64,512]{1,0:T(8,128)S(1)}, u32[]{:S(2)}, u32[]{:S(2)}) collective-permute-start(f32[64,512]{1,0:T(8,128)S(1)} %get-tuple-element.21.refs_0_), channel_id=1, source_target_pairs={{2,4},{3,5},{4,2},{5,3},{10,12},{11,13},{12,10},{13,11},{18,20},{1... | collective-permute-start | bytes 393224 | tf_op jit(solution)/shard_map/ppermute | solution.py:355
  34.1 13.5 %collective-permute-start.10 = (f32[64,1024]{1,0:T(8,128)S(1)}, f32[64,1024]{1,0:T(8,128)S(1)}, u32[]{:S(2)}, u32[]{:S(2)}) collective-permute-start(f32[64,1024]{1,0:T(8,128)S(1)} %get-tuple-element.26.refs_0_), channel_id=1, source_target_pairs={{0,24},{8,16},{16,8},{24,0},{1,25},{9,17},{17,9},{25,1},{2,26},{10... | collective-permute-start | bytes 786440 | tf_op jit(solution)/shard_map/ppermute | solution.py:358
  35.2 13.3 %collective-permute-start.8 = (f32[64,1024]{1,0:T(8,128)S(1)}, f32[64,1024]{1,0:T(8,128)S(1)}, u32[]{:S(2)}, u32[]{:S(2)}) collective-permute-start(f32[64,1024]{1,0:T(8,128)S(1)} %get-tuple-element.26.refs_0_), channel_id=1, source_target_pairs={{0,8},{8,0},{16,24},{24,16},{1,9},{9,1},{17,25},{25,17},{2,10},{10... | collective-permute-start | bytes 786440 | tf_op jit(solution)/shard_map/ppermute | solution.py:358
  36.7 13.9 %collective-permute-start.9 = (f32[64,1024]{1,0:T(8,128)S(1)}, f32[64,1024]{1,0:T(8,128)S(1)}, u32[]{:S(2)}, u32[]{:S(2)}) collective-permute-start(f32[64,1024]{1,0:T(8,128)S(1)} %get-tuple-element.26.refs_0_), channel_id=1, source_target_pairs={{0,16},{8,24},{16,0},{24,8},{1,17},{9,25},{17,1},{25,9},{2,18},{10... | collective-permute-start | bytes 786440 | tf_op jit(solution)/shard_map/ppermute | solution.py:358
  38.3 8.1 %collective-permute-start.3 = (f32[64,512]{1,0:T(8,128)S(1)}, f32[64,512]{1,0:T(8,128)S(1)}, u32[]{:S(2)}, u32[]{:S(2)}) collective-permute-start(f32[64,512]{1,0:T(8,128)S(1)} %collective-permute-done.1.refs_2_), channel_id=1, source_target_pairs={{2,0},{3,1},{4,6},{5,7},{10,8},{11,9},{12,14},{13,15},{18,16},{19,... | collective-permute-start | bytes 393224 | tf_op jit(solution)/shard_map/ppermute | solution.py:355
  46.9 5.3 %collective-permute-start.4 = (f32[64,512]{1,0:T(8,128)S(1)}, f32[64,512]{1,0:T(8,128)S(1)}, u32[]{:S(2)}, u32[]{:S(2)}) collective-permute-start(f32[64,512]{1,0:T(8,128)S(1)} %get-tuple-element.23), channel_id=1, source_target_pairs={{0,8},{8,0},{16,24},{24,16},{1,9},{9,1},{17,25},{25,17},{2,10},{10... | collective-permute-start | bytes 393224 | tf_op jit(solution)/shard_map/ppermute | solution.py:358
  47.5 5.7 %collective-permute-start.5 = (f32[64,512]{1,0:T(8,128)S(1)}, f32[64,512]{1,0:T(8,128)S(1)}, u32[]{:S(2)}, u32[]{:S(2)}) collective-permute-start(f32[64,512]{1,0:T(8,128)S(1)} %get-tuple-element.24), channel_id=1, source_target_pairs={{0,16},{8,24},{16,0},{24,8},{1,17},{9,25},{17,1},{25,9},{2,18},{10... | collective-permute-start | bytes 393224 | tf_op jit(solution)/shard_map/ppermute | solution.py:358
  48.4 7.0 %copy-start = (f32[64,32,128]{2,1,0:T(8,128)S(1)}, f32[64,32,128]{2,1,0:T(8,128)}, u32[]{:S(2)}) copy-start(f32[64,32,128]{2,1,0:T(8,128)} %refs_10_.3) | copy-start | bytes 3145732
  48.4 7.0 %copy-start.4 = (f32[512]{0:T(512)S(1)}, f32[512]{0:T(512)}, u32[]{:S(2)}) copy-start(f32[512]{0:T(512)} %param.25) | copy-start | bytes 6148
  48.4 7.0 %copy-start.5 = (f32[128]{0:T(128)S(1)}, f32[128]{0:T(128)}, u32[]{:S(2)}) copy-start(f32[128]{0:T(128)} %param.20) | copy-start | bytes 1540
  48.4 7.0 %copy-start.6 = (f32[128]{0:T(128)S(1)}, f32[128]{0:T(128)}, u32[]{:S(2)}) copy-start(f32[128]{0:T(128)} %param.22) | copy-start | bytes 1540
  48.4 7.0 %copy-start.7 = (f32[128]{0:T(128)S(1)}, f32[128]{0:T(128)}, u32[]{:S(2)}) copy-start(f32[128]{0:T(128)} %param.23) | copy-start | bytes 1540
  48.5 7.0 %copy-start.8 = (f32[128]{0:T(128)S(1)}, f32[128]{0:T(128)}, u32[]{:S(2)}) copy-start(f32[128]{0:T(128)} %param.27) | copy-start | bytes 1540
  48.5 6.8 %collective-permute-start.6 = (f32[64,512]{1,0:T(8,128)S(1)}, f32[64,512]{1,0:T(8,128)S(1)}, u32[]{:S(2)}, u32[]{:S(2)}) collective-permute-start(f32[64,512]{1,0:T(8,128)S(1)} %get-tuple-element.25), channel_id=1, source_target_pairs={{0,24},{8,16},{16,8},{24,0},{1,25},{9,17},{17,9},{25,1},{2,26},{10... | collective-permute-start | bytes 393224 | tf_op jit(solution)/shard_map/ppermute | solution.py:358
  55.3 13.5 %collective-permute-start.7 = (f32[256,512]{1,0:T(8,128)S(1)}, f32[256,512]{1,0:T(8,128)S(1)}, u32[]{:S(2)}, u32[]{:S(2)}) collective-permute-start(f32[256,512]{1,0:T(8,128)S(1)} %pack.2.refs_0_), channel_id=1, source_target_pairs={{0,1},{1,0},{2,3},{3,2},{4,5},{5,4},{6,7},{7,6},{8,9},{9,8},{10,11... | collective-permute-start | bytes 1572872 | tf_op jit(solution)/shard_map/ppermute | solution.py:361
where the time goes:
time: 74.8 us; the launch traced here: 73.6 us
  Pallas kernels  26.2 us (35%)
  starting transfers between devices  24.4 us (33%)
  waiting for transfers between devices  22.7 us (30%)
    pallas_call x3, Pallas kernels, pair_update(): pl.pallas_call(functools.partial(pair_kernel, len(lefts), steps, tile, wi...  18.1 us
    ppermute x8, waiting for transfers between devices, along_groups(): lax.ppermute(value, 'col', [(a * fold + k, b * fold + k) for a, b in pair...  17.1 us
    ppermute x8, starting transfers between devices, along_groups(): lax.ppermute(value, 'col', [(a * fold + k, b * fold + k) for a, b in pair...  13.3 us
    ppermute x9, starting transfers between devices, along_rows(): return lax.ppermute(value, 'row', [(a, a ^ m) for a in range(rows)])  10.9 us
    ppermute x9, waiting for transfers between devices, along_rows(): return lax.ppermute(value, 'row', [(a, a ^ m) for a in range(rows)])  5.62 us
    pallas_call x1, Pallas kernels, project(): pl.pallas_call(functools.partial(project_kernel, seqs, residues, width, c...  5.45 us
  transfers between devices with their start and end apart: 19, of which 9 were waited for; matrix products, arithmetic and copies ran while one was open for 0% of the time, Pallas kernels for 21%

commit v1 on v0

--- a/solution.py
+++ b/solution.py
@@ -34,7 +34,7 @@
 
 def project_kernel(seqs, residues, width, chunks, x_hbm, gain_hbm, bias_hbm, lw_hbm, rw_hbm, *refs):
     left_refs, right_ref, place_ref = refs[:chunks], refs[chunks], refs[chunks + 1]
-    x_ref, gain_ref, bias_ref, lw_ref, rw_ref, sems, w_high, w_low, y_ref, high_ref, low_ref = refs[chunks + 2 :]
+    x_ref, gain_ref, bias_ref, lw_ref, rw_ref, sems, w_ref, p_ref = refs[chunks + 2 :]
     fold = lax.axis_size("col") // lax.axis_size("row")
     col = lax.axis_index("col")
     place_ref[0] = jnp.bitwise_xor(lax.div(col, fold), lax.axis_index("row")).astype(jnp.int32)
@@ -54,35 +54,40 @@
         copy.start()
     for copy in copies[: len(small)]:
         copy.wait()
-    for at, ref in enumerate((lw_ref, rw_ref)):
-        for e in range(per):
-            zeros = [jnp.zeros((n * width, channels), F32) for n in (e, per - 1 - e)]
-            placed = jnp.concatenate([z for z in (zeros[0], ref[...], zeros[1]) if z.shape[0]], axis=0)
-            high, low = split(placed.T)
-            w_high[e * channels : (e + 1) * channels, at * LANES : (at + 1) * LANES] = high
-            w_low[e * channels : (e + 1) * channels, at * LANES : (at + 1) * LANES] = low
-
+    plain = jnp.concatenate([lw_ref[...], rw_ref[...]], axis=0)
+    high, low = split(jnp.concatenate([plain * gain_ref[...], plain], axis=0).T)
+    w_ref[:, :LANES] = high
+    w_ref[:, LANES:] = low
+
+    def multiply(values):
+        high, low = split(values)
+        both = dot(high, w_ref[...])
+        return both[:, :LANES] + both[:, LANES:] + dot(low, w_ref[:, :LANES])
+
+    offset = multiply(jnp.broadcast_to(bias_ref[...], (8, channels)))
+    offset = pltpu.roll(offset, LANES - 2 * width, 1)[:1]
+    lane = lax.broadcasted_iota(jnp.int32, (seqs, LANES), 1) // width
+    share = groups // chunks
     for step in range(steps):
         copies[len(small) + step].wait()
-        normed = norm(x_ref[step * block : (step + 1) * block, :], gain_ref[...], bias_ref[...])
-        for part in range(channels // LANES):
-            y_ref[step, part] = normed[:, part * LANES : (part + 1) * LANES]
-        for e in range(per):
-            for g in range(groups):
-                for part in range(channels // LANES):
-                    high, low = split(y_ref[step, part, pl.ds(g * per + e, seqs, stride=residues), :])
-                    first = e * channels + part * LANES
-                    high_ref[step, g * seqs : (g + 1) * seqs, first : first + LANES] = high
-                    low_ref[step, g * seqs : (g + 1) * seqs, first : first + LANES] = low
-        high, low = high_ref[step], low_ref[step]
-        both = dot(high, w_high[...]) + dot(low, w_high[...]) + dot(high, w_low[...])
-        share = groups // chunks
+        x = x_ref[step * block : (step + 1) * block, :]
+        centred = x - jnp.mean(x, axis=-1, keepdims=True)
+        spread = jnp.mean(jnp.square(centred), axis=-1, keepdims=True)
+        p_ref[step] = multiply(centred) * lax.rsqrt(spread + EPS) + offset
+        to = slice(step * seqs, (step + 1) * seqs)
         for g in range(groups):
-            rows = both[g * seqs : (g + 1) * seqs]
-            to = slice(step * seqs, (step + 1) * seqs)
-            at = g % share
-            left_refs[g // share][to, at * LANES : (at + 1) * LANES] = rows[:, :LANES]
-            right_ref[to, g * LANES : (g + 1) * LANES] = rows[:, LANES:]
+            rows = [p_ref[step, pl.ds(g * per + e, seqs, stride=residues), :] for e in range(per)]
+            for side in range(2):
+                value = None
+                for e in range(per):
+                    shift = (e - side) % per * width
+                    placed = pltpu.roll(rows[e], shift, 1) if shift else rows[e]
+                    value = placed if value is None else jnp.where(lane == e, placed, value)
+                if side:
+                    right_ref[to, g * LANES : (g + 1) * LANES] = value
+                else:
+                    at = g % share
+                    left_refs[g // share][to, at * LANES : (at + 1) * LANES] = value
 
 
 def project(alignment, gain, bias, left_weight, right_weight, chunks):
@@ -90,8 +95,6 @@
     width = left_weight.shape[1]
     steps = 4
     seqs = seq_local // steps
-    per = LANES // width
-    groups = residues // per
     span = residues * width
     outs = [jax.ShapeDtypeStruct((seq_local, span // chunks), F32)] * chunks + [
         jax.ShapeDtypeStruct((seq_local, span), F32),
@@ -109,11 +112,8 @@
             pltpu.VMEM((width, channels), F32),
             pltpu.VMEM((width, channels), F32),
             pltpu.SemaphoreType.DMA((4 + steps,)),
-            pltpu.VMEM((per * channels, 2 * LANES), BF16),
-            pltpu.VMEM((per * channels, 2 * LANES), BF16),
-            pltpu.VMEM((steps, channels // LANES, seqs * residues, LANES), F32),
-            pltpu.VMEM((steps, groups * seqs, per * channels), BF16),
-            pltpu.VMEM((steps, groups * seqs, per * channels), BF16),
+            pltpu.VMEM((channels, 2 * LANES), BF16),
+            pltpu.VMEM((steps, seqs * residues, LANES), F32),
         ],
         cost_estimate=pl.CostEstimate(flops=6 * 10**9, bytes_accessed=4 * 10**6, transcendentals=0),
         compiler_params=pltpu.CompilerParams(vmem_limit_bytes=VMEM),
@@ -281,7 +281,7 @@
 
 
 def pair_update(place, members, chunk, lefts, rt, weights, vectors, pair_state, out, width):
-    tile = 8
+    tile = 16
     wp, wh, wf = weights
     seqs, span = lefts[0].shape
     steps = span // (tile * width)

time: 74.8 us -> 67.8 us (0.906); the launches traced: 73.6 us -> 67.6 us
  Pallas kernels: 26.2 us -> 20.2 us
  starting transfers between devices: 24.4 us -> 23.6 us
    ppermute x9, waiting for transfers between devices: 5.62 us -> 15.7 us  [along_rows(): return lax.ppermute(value, 'row', [(a, a ^ m) for a in range(rows)])]
    ppermute x8, waiting for transfers between devices: 17.1 us -> 7.64 us  [along_groups(): lax.ppermute(value, 'col', [(a * fold + k, b * fold + k) for a, b in pair...]
    pallas_call x3, Pallas kernels: 18.1 us -> 13.9 us  [pair_update(): pl.pallas_call(functools.partial(pair_kernel, len(lefts), steps, tile, wi...]
    pallas_call x1, Pallas kernels: 5.45 us -> 3.41 us  [project(): pl.pallas_call(functools.partial(project_kernel, seqs, residues, width, c...]
  transfers between devices with their start and end apart: 19 -> 19, of which waited for: 9 -> 6; matrix products, arithmetic and copies ran while one was open for 0% -> 0% of each run, Pallas kernels for 21% -> 19%
where the time goes in v1:
time: 67.8 us; the launch traced here: 67.6 us
  starting transfers between devices  23.6 us (35%)
  waiting for transfers between devices  23.4 us (35%)
  Pallas kernels  20.2 us (30%)
    ppermute x9, waiting for transfers between devices, along_rows(): return lax.ppermute(value, 'row', [(a, a ^ m) for a in range(rows)])  15.7 us
    pallas_call x3, Pallas kernels, pair_update(): pl.pallas_call(functools.partial(pair_kernel, len(lefts), steps, tile, wi...  13.9 us
    ppermute x8, starting transfers between devices, along_groups(): lax.ppermute(value, 'col', [(a * fold + k, b * fold + k) for a, b in pair...  12.6 us
    ppermute x9, starting transfers between devices, along_rows(): return lax.ppermute(value, 'row', [(a, a ^ m) for a in range(rows)])  10.8 us
    ppermute x8, waiting for transfers between devices, along_groups(): lax.ppermute(value, 'col', [(a * fold + k, b * fold + k) for a, b in pair...  7.64 us
    pallas_call x1, Pallas kernels, project(): pl.pallas_call(functools.partial(project_kernel, seqs, residues, width, c...  3.41 us
    pallas_call x2, Pallas kernels, route(): pl.pallas_call(functools.partial(route_kernel, slots), out_shape=[jax.Sha...  1.39 us
  transfers between devices with their start and end apart: 19, of which 6 were waited for; matrix products, arithmetic and copies ran while one was open for 0% of the time, Pallas kernels for 19%

profile of v1, /device:TPU:0, one launch (start us, length us, event | category | flops | bytes accessed | tf_op | source)
XLA Modules:
  0.0 67.6 jit_solution(7082652174265986469)
XLA Ops:
  0.0 3.4 %project.1 = (f32[64,512]{1,0:T(8,128)S(1)}, f32[64,512]{1,0:T(8,128)S(1)}, f32[64,1024]{1,0:T(8,128)S(1)}, s32[2]{0:T(128)S(1)}) custom-call(f32[2048,256]{1,0:T(8,128)} %bitcast.25, f32[1,256]{1,0:T(1,128)} %bitcast.28, f32[1,256]{1,0:T(1,128)} %bitcast.29, f32[32,256]{1,0:T(8,128)} %bitcast.26, f32[32,256]{1,0:T(8,128)} %bitcast.27), custom_call_target="tpu_custom_call" | custom-call | flops 6000000000 | bytes 4000000 | tf_op jit(solution)/shard_map/project/pallas_call | solution.py:103
  3.4 0.0 copy-start.6
  3.4 0.0 copy-start.7
  3.4 0.0 copy-start.8
  3.5 4.1 %collective-permute-start.12 = (f32[64,512]{1,0:T(8,128)S(1)}, f32[64,512]{1,0:T(8,128)S(1)}, u32[]{:S(2)}, u32[]{:S(2)}) collective-permute-start(f32[64,512]{1,0:T(8,128)S(1)} %get-tuple-element.30.refs_0_), channel_id=1, source_target_pairs={{0,4},{1,5},{2,6},{3,7},{4,0},{5,1},{6,2},{7,3},{8,12},{9,13},{10,... | collective-permute-start | bytes 393224 | tf_op jit(solution)/shard_map/ppermute | solution.py:355
  7.6 1.6 %collective-permute-start.11 = (f32[64,512]{1,0:T(8,128)S(1)}, f32[64,512]{1,0:T(8,128)S(1)}, u32[]{:S(2)}, u32[]{:S(2)}) collective-permute-start(f32[64,512]{1,0:T(8,128)S(1)} %get-tuple-element.30.refs_0_), channel_id=1, source_target_pairs={{0,2},{1,3},{2,0},{3,1},{4,6},{5,7},{6,4},{7,5},{8,10},{9,11},{10,... | collective-permute-start | bytes 393224 | tf_op jit(solution)/shard_map/ppermute | solution.py:355
  9.2 0.3 collective-permute-start.1
  9.5 0.7 collective-permute-start.13
  10.2 5.4 %collective-permute-done.12.refs_2_ = f32[64,512]{1,0:T(8,128)S(1)} collective-permute-done((f32[64,512]{1,0:T(8,128)S(1)}, f32[64,512]{1,0:T(8,128)S(1)}, u32[]{:S(2)}, u32[]{:S(2)}) %collective-permute-start.12) | collective-permute-done | bytes 131104 | tf_op jit(solution)/shard_map/ppermute | solution.py:355
  15.6 1.3 %collective-permute-start.14 = (f32[64,512]{1,0:T(8,128)S(1)}, f32[64,512]{1,0:T(8,128)S(1)}, u32[]{:S(2)}, u32[]{:S(2)}) collective-permute-start(f32[64,512]{1,0:T(8,128)S(1)} %collective-permute-done.12.refs_2_), channel_id=1, source_target_pairs={{2,0},{3,1},{4,6},{5,7},{10,8},{11,9},{12,14},{13,15},{18,16},{19,... | collective-permute-start | bytes 393224 | tf_op jit(solution)/shard_map/ppermute | solution.py:355
  16.9 2.7 %collective-permute-start = (f32[64,512]{1,0:T(8,128)S(1)}, f32[64,512]{1,0:T(8,128)S(1)}, u32[]{:S(2)}, u32[]{:S(2)}) collective-permute-start(f32[64,512]{1,0:T(8,128)S(1)} %get-tuple-element.21.refs_0_), channel_id=1, source_target_pairs={{0,2},{1,3},{2,0},{3,1},{4,6},{5,7},{6,4},{7,5},{8,10},{9,11},{10,... | collective-permute-start | bytes 393224 | tf_op jit(solution)/shard_map/ppermute | solution.py:355
  19.6 0.0 collective-permute-done.11.refs_1_
  19.6 0.7 collective-permute-start.2
  20.2 0.1 collective-permute-done.1.refs_2_
  20.4 1.3 %collective-permute-start.3 = (f32[64,512]{1,0:T(8,128)S(1)}, f32[64,512]{1,0:T(8,128)S(1)}, u32[]{:S(2)}, u32[]{:S(2)}) collective-permute-start(f32[64,512]{1,0:T(8,128)S(1)} %collective-permute-done.1.refs_2_), channel_id=1, source_target_pairs={{2,0},{3,1},{4,6},{5,7},{10,8},{11,9},{12,14},{13,15},{18,16},{19,... | collective-permute-start | bytes 393224 | tf_op jit(solution)/shard_map/ppermute | solution.py:355
  21.7 0.0 collective-permute-done.13.refs_3_
  21.7 1.5 %collective-permute-done.14.refs_4_ = f32[64,512]{1,0:T(8,128)S(1)} collective-permute-done((f32[64,512]{1,0:T(8,128)S(1)}, f32[64,512]{1,0:T(8,128)S(1)}, u32[]{:S(2)}, u32[]{:S(2)}) %collective-permute-start.14) | collective-permute-done | bytes 131104 | tf_op jit(solution)/shard_map/ppermute | solution.py:355
  23.2 0.6 route.3
  23.8 1.5 %collective-permute-start.15 = (f32[64,512]{1,0:T(8,128)S(1)}, f32[64,512]{1,0:T(8,128)S(1)}, u32[]{:S(2)}, u32[]{:S(2)}) collective-permute-start(f32[64,512]{1,0:T(8,128)S(1)} %get-tuple-element.32), channel_id=1, source_target_pairs={{0,8},{8,0},{16,24},{24,16},{1,9},{9,1},{17,25},{25,17},{2,10},{10... | collective-permute-start | bytes 393224 | tf_op jit(solution)/shard_map/ppermute | solution.py:358
  25.3 1.5 %collective-permute-start.16 = (f32[64,512]{1,0:T(8,128)S(1)}, f32[64,512]{1,0:T(8,128)S(1)}, u32[]{:S(2)}, u32[]{:S(2)}) collective-permute-start(f32[64,512]{1,0:T(8,128)S(1)} %get-tuple-element.33), channel_id=1, source_target_pairs={{0,16},{8,24},{16,0},{24,8},{1,17},{9,25},{17,1},{25,9},{2,18},{10... | collective-permute-start | bytes 393224 | tf_op jit(solution)/shard_map/ppermute | solution.py:358
  26.8 0.0 collective-permute-done.refs_1_
  26.8 0.5 collective-permute-start.17
  27.4 0.0 collective-permute-done.2.refs_3_
  27.4 0.6 collective-permute-done.3.refs_4_
  27.9 0.8 %route.2 = (f32[64,512]{1,0:T(8,128)S(1)}, f32[64,512]{1,0:T(8,128)S(1)}, f32[64,512]{1,0:T(8,128)S(1)}, f32[64,512]{1,0:T(8,128)S(1)}) custom-call(s32[2]{0:T(128)S(1)} %get-tuple-element.20.t_ref.at_ref, f32[64,512]{1,0:T(8,128)S(1)} %get-tuple-element.21.refs_0_, f32[64,512]{1,0:T(8,128)S(1)} %collective-permute-done.refs_1_, ...), custom_call_target="tpu_custom_call" | custom-call | flops 1000000 | bytes 2000000 | tf_op jit(solution)/shard_map/route/pallas_call | solution.py:211
  28.7 1.6 %collective-permute-start.4 = (f32[64,512]{1,0:T(8,128)S(1)}, f32[64,512]{1,0:T(8,128)S(1)}, u32[]{:S(2)}, u32[]{:S(2)}) collective-permute-start(f32[64,512]{1,0:T(8,128)S(1)} %get-tuple-element.23), channel_id=1, source_target_pairs={{0,8},{8,0},{16,24},{24,16},{1,9},{9,1},{17,25},{25,17},{2,10},{10... | collective-permute-start | bytes 393224 | tf_op jit(solution)/shard_map/ppermute | solution.py:358
  30.3 1.5 %collective-permute-start.5 = (f32[64,512]{1,0:T(8,128)S(1)}, f32[64,512]{1,0:T(8,128)S(1)}, u32[]{:S(2)}, u32[]{:S(2)}) collective-permute-start(f32[64,512]{1,0:T(8,128)S(1)} %get-tuple-element.24), channel_id=1, source_target_pairs={{0,16},{8,24},{16,0},{24,8},{1,17},{9,25},{17,1},{25,9},{2,18},{10... | collective-permute-start | bytes 393224 | tf_op jit(solution)/shard_map/ppermute | solution.py:358
  31.8 0.0 collective-permute-done.15.refs_1_
  31.8 0.0 collective-permute-done.16.refs_2_
  31.8 1.8 %collective-permute-done.17.refs_3_ = f32[64,512]{1,0:T(8,128)S(1)} collective-permute-done((f32[64,512]{1,0:T(8,128)S(1)}, f32[64,512]{1,0:T(8,128)S(1)}, u32[]{:S(2)}, u32[]{:S(2)}) %collective-permute-start.17) | collective-permute-done | bytes 131104 | tf_op jit(solution)/shard_map/ppermute | solution.py:358
  33.7 0.1 collective-permute-start.18
  33.8 0.7 %collective-permute-start.10 = (f32[64,1024]{1,0:T(8,128)S(1)}, f32[64,1024]{1,0:T(8,128)S(1)}, u32[]{:S(2)}, u32[]{:S(2)}) collective-permute-start(f32[64,1024]{1,0:T(8,128)S(1)} %get-tuple-element.26.refs_0_), channel_id=1, source_target_pairs={{0,24},{8,16},{16,8},{24,0},{1,25},{9,17},{17,9},{25,1},{2,26},{10... | collective-permute-start | bytes 786440 | tf_op jit(solution)/shard_map/ppermute | solution.py:358
  34.5 1.3 %collective-permute-start.8 = (f32[64,1024]{1,0:T(8,128)S(1)}, f32[64,1024]{1,0:T(8,128)S(1)}, u32[]{:S(2)}, u32[]{:S(2)}) collective-permute-start(f32[64,1024]{1,0:T(8,128)S(1)} %get-tuple-element.26.refs_0_), channel_id=1, source_target_pairs={{0,8},{8,0},{16,24},{24,16},{1,9},{9,1},{17,25},{25,17},{2,10},{10... | collective-permute-start | bytes 786440 | tf_op jit(solution)/shard_map/ppermute | solution.py:358
  35.8 0.0 collective-permute-done.4.refs_1_
  35.8 1.5 %collective-permute-start.9 = (f32[64,1024]{1,0:T(8,128)S(1)}, f32[64,1024]{1,0:T(8,128)S(1)}, u32[]{:S(2)}, u32[]{:S(2)}) collective-permute-start(f32[64,1024]{1,0:T(8,128)S(1)} %get-tuple-element.26.refs_0_), channel_id=1, source_target_pairs={{0,16},{8,24},{16,0},{24,8},{1,17},{9,25},{17,1},{25,9},{2,18},{10... | collective-permute-start | bytes 786440 | tf_op jit(solution)/shard_map/ppermute | solution.py:358
  37.3 0.0 collective-permute-done.5.refs_2_
  37.3 0.6 collective-permute-start.6
  38.0 13.9 %collective-permute-done.6.refs_3_ = f32[64,512]{1,0:T(8,128)S(1)} collective-permute-done((f32[64,512]{1,0:T(8,128)S(1)}, f32[64,512]{1,0:T(8,128)S(1)}, u32[]{:S(2)}, u32[]{:S(2)}) %collective-permute-start.6) | collective-permute-done | bytes 131104 | tf_op jit(solution)/shard_map/ppermute | solution.py:358
  51.9 0.1 collective-permute-start.7
  52.0 0.0 copy-done.6
  52.0 0.0 copy-done.7
  52.0 0.0 copy-done.8
  52.0 0.4 weights.1
  52.4 0.0 copy-start
  52.5 0.0 copy-start.1
  52.5 0.0 copy-start.2
  52.5 0.0 copy-start.3
  52.5 0.0 copy-start.4
  52.5 0.0 copy-start.5
  52.5 0.0 collective-permute-done.10.refs_3_
  52.5 0.0 collective-permute-done.8.refs_1_
  52.5 0.0 collective-permute-done.9.refs_2_
  52.5 1.0 %turn.1.refs_2_.refs_1_ = bf16[1024,768]{1,0:T(8,128)(2,1)S(1)} custom-call(f32[64,1024]{1,0:T(8,128)S(1)} %get-tuple-element.26.refs_0_, f32[64,1024]{1,0:T(8,128)S(1)} %collective-permute-done.8.refs_1_, f32[64,1024]{1,0:T(8,128)S(1)} %collective-permute-done.9.refs_2_, f32[64,1024]{1,0:T(8,128)S(1)} %collective-permute-done.10.refs_3_), custom_call_target="tpu_custom_call" | custom-call | flops 2000000000 | bytes 3000000 | tf_op jit(solution)/shard_map/turn/pallas_call | solution.py:184
  53.5 0.0 collective-permute-done.18.refs_1_
  53.5 0.1 copy-done
  53.7 0.0 copy-done.1
  53.7 0.0 copy-done.2
  53.7 0.0 copy-done.3
  53.7 0.0 copy-done.4
  53.7 0.0 copy-done.5
  53.7 6.4 %pair.3.refs_11_ = f32[64,32,128]{2,1,0:T(8,128)} custom-call(s32[2]{0:T(128)S(1)} %get-tuple-element.20.t_ref.at_ref, f32[256,512]{1,0:T(8,128)S(1)} %pack.3.refs_0_, f32[256,512]{1,0:T(8,128)S(1)} %collective-permute-done.18.refs_1_, bf16[1024,768]{1,0:T(8,128)(2,1)S(1)} %turn.1.refs_2_.refs_1_, bf16[1024,256]{1,0:T(8,128)(2,1)S(1)} %get-tuple-element.27.refs_3_.refs_2_, ...), custom_call_target="tpu_custom_call" | custom-call | flops 2000000000 | bytes 4000000 | tf_op jit(solution)/shard_map/pair/pallas_call | solution.py:311
  60.1 3.8 %pair.4.refs_11_ = f32[64,32,128]{2,1,0:T(8,128)} custom-call(s32[2]{0:T(128)S(1)} %get-tuple-element.20.t_ref.at_ref, f32[256,512]{1,0:T(8,128)S(1)} %pack.2.refs_0_, bf16[1024,768]{1,0:T(8,128)(2,1)S(1)} %turn.1.refs_2_.refs_1_, bf16[1024,256]{1,0:T(8,128)(2,1)S(1)} %get-tuple-element.27.refs_3_.refs_2_, ...), custom_call_target="tpu_custom_call", output_to_operand_aliasing={{}: (12, {})} | custom-call | flops 1000000000 | bytes 4000000 | tf_op jit(solution)/shard_map/pair/pallas_call | solution.py:311
  63.8 0.0 collective-permute-done.7.refs_0_
  63.8 3.8 %pair.5 = f32[64,32,128]{2,1,0:T(8,128)} custom-call(s32[2]{0:T(128)S(1)} %get-tuple-element.20.t_ref.at_ref, f32[256,512]{1,0:T(8,128)S(1)} %collective-permute-done.7.refs_0_, bf16[1024,768]{1,0:T(8,128)(2,1)S(1)} %turn.1.refs_2_.refs_1_, bf16[1024,256]{1,0:T(8,128)(2,1)S(1)} %get-tuple-element.27.refs_3_.refs_2_, ...), custom_call_target="tpu_custom_call", output_to_operand_aliasing={{}: (12, {})} | custom-call | flops 1000000000 | bytes 4000000 | tf_op jit(solution)/shard_map/pair/pallas_call | solution.py:311
  (2 shorter events, 0.1 us)
Async XLA Ops:
  3.4 48.5 %copy-start.6 = (f32[1024,128]{1,0:T(8,128)S(1)}, f32[1024,128]{1,0:T(8,128)}, u32[]{:S(2)}) copy-start(f32[1024,128]{1,0:T(8,128)} %wp_ref.1) | copy-start | bytes 1572868
  3.4 48.5 %copy-start.7 = (f32[128,512]{1,0:T(8,128)S(1)}, f32[128,512]{1,0:T(8,128)}, u32[]{:S(2)}) copy-start(f32[128,512]{1,0:T(8,128)} %wh_ref.1) | copy-start | bytes 786436
  3.4 48.5 %copy-start.8 = (f32[512,128]{1,0:T(8,128)S(1)}, f32[512,128]{1,0:T(8,128)}, u32[]{:S(2)}) copy-start(f32[512,128]{1,0:T(8,128)} %wf_ref.1) | copy-start | bytes 786436
  3.5 12.1 %collective-permute-start.12 = (f32[64,512]{1,0:T(8,128)S(1)}, f32[64,512]{1,0:T(8,128)S(1)}, u32[]{:S(2)}, u32[]{:S(2)}) collective-permute-start(f32[64,512]{1,0:T(8,128)S(1)} %get-tuple-element.30.refs_0_), channel_id=1, source_target_pairs={{0,4},{1,5},{2,6},{3,7},{4,0},{5,1},{6,2},{7,3},{8,12},{9,13},{10,... | collective-permute-start | bytes 393224 | tf_op jit(solution)/shard_map/ppermute | solution.py:355
  7.6 12.0 %collective-permute-start.11 = (f32[64,512]{1,0:T(8,128)S(1)}, f32[64,512]{1,0:T(8,128)S(1)}, u32[]{:S(2)}, u32[]{:S(2)}) collective-permute-start(f32[64,512]{1,0:T(8,128)S(1)} %get-tuple-element.30.refs_0_), channel_id=1, source_target_pairs={{0,2},{1,3},{2,0},{3,1},{4,6},{5,7},{6,4},{7,5},{8,10},{9,11},{10,... | collective-permute-start | bytes 393224 | tf_op jit(solution)/shard_map/ppermute | solution.py:355
  9.2 11.2 %collective-permute-start.1 = (f32[64,512]{1,0:T(8,128)S(1)}, f32[64,512]{1,0:T(8,128)S(1)}, u32[]{:S(2)}, u32[]{:S(2)}) collective-permute-start(f32[64,512]{1,0:T(8,128)S(1)} %get-tuple-element.21.refs_0_), channel_id=1, source_target_pairs={{0,4},{1,5},{2,6},{3,7},{4,0},{5,1},{6,2},{7,3},{8,12},{9,13},{10,... | collective-permute-start | bytes 393224 | tf_op jit(solution)/shard_map/ppermute | solution.py:355
  9.5 12.2 %collective-permute-start.13 = (f32[64,512]{1,0:T(8,128)S(1)}, f32[64,512]{1,0:T(8,128)S(1)}, u32[]{:S(2)}, u32[]{:S(2)}) collective-permute-start(f32[64,512]{1,0:T(8,128)S(1)} %get-tuple-element.30.refs_0_), channel_id=1, source_target_pairs={{2,4},{3,5},{4,2},{5,3},{10,12},{11,13},{12,10},{13,11},{18,20},{1... | collective-permute-start | bytes 393224 | tf_op jit(solution)/shard_map/ppermute | solution.py:355
  15.6 7.6 %collective-permute-start.14 = (f32[64,512]{1,0:T(8,128)S(1)}, f32[64,512]{1,0:T(8,128)S(1)}, u32[]{:S(2)}, u32[]{:S(2)}) collective-permute-start(f32[64,512]{1,0:T(8,128)S(1)} %collective-permute-done.12.refs_2_), channel_id=1, source_target_pairs={{2,0},{3,1},{4,6},{5,7},{10,8},{11,9},{12,14},{13,15},{18,16},{19,... | collective-permute-start | bytes 393224 | tf_op jit(solution)/shard_map/ppermute | solution.py:355
  16.9 10.0 %collective-permute-start = (f32[64,512]{1,0:T(8,128)S(1)}, f32[64,512]{1,0:T(8,128)S(1)}, u32[]{:S(2)}, u32[]{:S(2)}) collective-permute-start(f32[64,512]{1,0:T(8,128)S(1)} %get-tuple-element.21.refs_0_), channel_id=1, source_target_pairs={{0,2},{1,3},{2,0},{3,1},{4,6},{5,7},{6,4},{7,5},{8,10},{9,11},{10,... | collective-permute-start | bytes 393224 | tf_op jit(solution)/shard_map/ppermute | solution.py:355
  19.6 7.8 %collective-permute-start.2 = (f32[64,512]{1,0:T(8,128)S(1)}, f32[64,512]{1,0:T(8,128)S(1)}, u32[]{:S(2)}, u32[]{:S(2)}) collective-permute-start(f32[64,512]{1,0:T(8,128)S(1)} %get-tuple-element.21.refs_0_), channel_id=1, source_target_pairs={{2,4},{3,5},{4,2},{5,3},{10,12},{11,13},{12,10},{13,11},{18,20},{1... | collective-permute-start | bytes 393224 | tf_op jit(solution)/shard_map/ppermute | solution.py:355
  20.4 7.6 %collective-permute-start.3 = (f32[64,512]{1,0:T(8,128)S(1)}, f32[64,512]{1,0:T(8,128)S(1)}, u32[]{:S(2)}, u32[]{:S(2)}) collective-permute-start(f32[64,512]{1,0:T(8,128)S(1)} %collective-permute-done.1.refs_2_), channel_id=1, source_target_pairs={{2,0},{3,1},{4,6},{5,7},{10,8},{11,9},{12,14},{13,15},{18,16},{19,... | collective-permute-start | bytes 393224 | tf_op jit(solution)/shard_map/ppermute | solution.py:355
  23.8 8.0 %collective-permute-start.15 = (f32[64,512]{1,0:T(8,128)S(1)}, f32[64,512]{1,0:T(8,128)S(1)}, u32[]{:S(2)}, u32[]{:S(2)}) collective-permute-start(f32[64,512]{1,0:T(8,128)S(1)} %get-tuple-element.32), channel_id=1, source_target_pairs={{0,8},{8,0},{16,24},{24,16},{1,9},{9,1},{17,25},{25,17},{2,10},{10... | collective-permute-start | bytes 393224 | tf_op jit(solution)/shard_map/ppermute | solution.py:358
  25.3 6.5 %collective-permute-start.16 = (f32[64,512]{1,0:T(8,128)S(1)}, f32[64,512]{1,0:T(8,128)S(1)}, u32[]{:S(2)}, u32[]{:S(2)}) collective-permute-start(f32[64,512]{1,0:T(8,128)S(1)} %get-tuple-element.33), channel_id=1, source_target_pairs={{0,16},{8,24},{16,0},{24,8},{1,17},{9,25},{17,1},{25,9},{2,18},{10... | collective-permute-start | bytes 393224 | tf_op jit(solution)/shard_map/ppermute | solution.py:358
  26.8 6.8 %collective-permute-start.17 = (f32[64,512]{1,0:T(8,128)S(1)}, f32[64,512]{1,0:T(8,128)S(1)}, u32[]{:S(2)}, u32[]{:S(2)}) collective-permute-start(f32[64,512]{1,0:T(8,128)S(1)} %get-tuple-element.34), channel_id=1, source_target_pairs={{0,24},{8,16},{16,8},{24,0},{1,25},{9,17},{17,9},{25,1},{2,26},{10... | collective-permute-start | bytes 393224 | tf_op jit(solution)/shard_map/ppermute | solution.py:358
  28.7 7.1 %collective-permute-start.4 = (f32[64,512]{1,0:T(8,128)S(1)}, f32[64,512]{1,0:T(8,128)S(1)}, u32[]{:S(2)}, u32[]{:S(2)}) collective-permute-start(f32[64,512]{1,0:T(8,128)S(1)} %get-tuple-element.23), channel_id=1, source_target_pairs={{0,8},{8,0},{16,24},{24,16},{1,9},{9,1},{17,25},{25,17},{2,10},{10... | collective-permute-start | bytes 393224 | tf_op jit(solution)/shard_map/ppermute | solution.py:358
  30.3 7.0 %collective-permute-start.5 = (f32[64,512]{1,0:T(8,128)S(1)}, f32[64,512]{1,0:T(8,128)S(1)}, u32[]{:S(2)}, u32[]{:S(2)}) collective-permute-start(f32[64,512]{1,0:T(8,128)S(1)} %get-tuple-element.24), channel_id=1, source_target_pairs={{0,16},{8,24},{16,0},{24,8},{1,17},{9,25},{17,1},{25,9},{2,18},{10... | collective-permute-start | bytes 393224 | tf_op jit(solution)/shard_map/ppermute | solution.py:358
  33.7 19.8 %collective-permute-start.18 = (f32[256,512]{1,0:T(8,128)S(1)}, f32[256,512]{1,0:T(8,128)S(1)}, u32[]{:S(2)}, u32[]{:S(2)}) collective-permute-start(f32[256,512]{1,0:T(8,128)S(1)} %pack.3.refs_0_), channel_id=1, source_target_pairs={{0,1},{1,0},{2,3},{3,2},{4,5},{5,4},{6,7},{7,6},{8,9},{9,8},{10,11... | collective-permute-start | bytes 1572872 | tf_op jit(solution)/shard_map/ppermute | solution.py:361
  33.8 18.8 %collective-permute-start.10 = (f32[64,1024]{1,0:T(8,128)S(1)}, f32[64,1024]{1,0:T(8,128)S(1)}, u32[]{:S(2)}, u32[]{:S(2)}) collective-permute-start(f32[64,1024]{1,0:T(8,128)S(1)} %get-tuple-element.26.refs_0_), channel_id=1, source_target_pairs={{0,24},{8,16},{16,8},{24,0},{1,25},{9,17},{17,9},{25,1},{2,26},{10... | collective-permute-start | bytes 786440 | tf_op jit(solution)/shard_map/ppermute | solution.py:358
  34.5 18.0 %collective-permute-start.8 = (f32[64,1024]{1,0:T(8,128)S(1)}, f32[64,1024]{1,0:T(8,128)S(1)}, u32[]{:S(2)}, u32[]{:S(2)}) collective-permute-start(f32[64,1024]{1,0:T(8,128)S(1)} %get-tuple-element.26.refs_0_), channel_id=1, source_target_pairs={{0,8},{8,0},{16,24},{24,16},{1,9},{9,1},{17,25},{25,17},{2,10},{10... | collective-permute-start | bytes 786440 | tf_op jit(solution)/shard_map/ppermute | solution.py:358
  35.8 16.7 %collective-permute-start.9 = (f32[64,1024]{1,0:T(8,128)S(1)}, f32[64,1024]{1,0:T(8,128)S(1)}, u32[]{:S(2)}, u32[]{:S(2)}) collective-permute-start(f32[64,1024]{1,0:T(8,128)S(1)} %get-tuple-element.26.refs_0_), channel_id=1, source_target_pairs={{0,16},{8,24},{16,0},{24,8},{1,17},{9,25},{17,1},{25,9},{2,18},{10... | collective-permute-start | bytes 786440 | tf_op jit(solution)/shard_map/ppermute | solution.py:358
  37.3 14.5 %collective-permute-start.6 = (f32[64,512]{1,0:T(8,128)S(1)}, f32[64,512]{1,0:T(8,128)S(1)}, u32[]{:S(2)}, u32[]{:S(2)}) collective-permute-start(f32[64,512]{1,0:T(8,128)S(1)} %get-tuple-element.25), channel_id=1, source_target_pairs={{0,24},{8,16},{16,8},{24,0},{1,25},{9,17},{17,9},{25,1},{2,26},{10... | collective-permute-start | bytes 393224 | tf_op jit(solution)/shard_map/ppermute | solution.py:358
  51.9 12.0 %collective-permute-start.7 = (f32[256,512]{1,0:T(8,128)S(1)}, f32[256,512]{1,0:T(8,128)S(1)}, u32[]{:S(2)}, u32[]{:S(2)}) collective-permute-start(f32[256,512]{1,0:T(8,128)S(1)} %pack.2.refs_0_), channel_id=1, source_target_pairs={{0,1},{1,0},{2,3},{3,2},{4,5},{5,4},{6,7},{7,6},{8,9},{9,8},{10,11... | collective-permute-start | bytes 1572872 | tf_op jit(solution)/shard_map/ppermute | solution.py:361
  52.4 1.2 %copy-start = (f32[64,32,128]{2,1,0:T(8,128)S(1)}, f32[64,32,128]{2,1,0:T(8,128)}, u32[]{:S(2)}) copy-start(f32[64,32,128]{2,1,0:T(8,128)} %refs_10_.3) | copy-start | bytes 3145732
  52.5 1.2 %copy-start.1 = (f32[512]{0:T(512)S(1)}, f32[512]{0:T(512)}, u32[]{:S(2)}) copy-start(f32[512]{0:T(512)} %param.25) | copy-start | bytes 6148
  52.5 1.2 %copy-start.2 = (f32[128]{0:T(128)S(1)}, f32[128]{0:T(128)}, u32[]{:S(2)}) copy-start(f32[128]{0:T(128)} %param.20) | copy-start | bytes 1540
  52.5 1.2 %copy-start.3 = (f32[128]{0:T(128)S(1)}, f32[128]{0:T(128)}, u32[]{:S(2)}) copy-start(f32[128]{0:T(128)} %param.22) | copy-start | bytes 1540
  52.5 1.2 %copy-start.4 = (f32[128]{0:T(128)S(1)}, f32[128]{0:T(128)}, u32[]{:S(2)}) copy-start(f32[128]{0:T(128)} %param.23) | copy-start | bytes 1540
  52.5 1.2 %copy-start.5 = (f32[128]{0:T(128)S(1)}, f32[128]{0:T(128)}, u32[]{:S(2)}) copy-start(f32[128]{0:T(128)} %param.27) | copy-start | bytes 1540

commit v2 on v1

--- a/solution.py
+++ b/solution.py
@@ -32,13 +32,9 @@
     return centred * lax.rsqrt(spread + EPS) * gain + offset
 
 
-def project_kernel(seqs, residues, width, chunks, x_hbm, gain_hbm, bias_hbm, lw_hbm, rw_hbm, *refs):
-    left_refs, right_ref, place_ref = refs[:chunks], refs[chunks], refs[chunks + 1]
-    x_ref, gain_ref, bias_ref, lw_ref, rw_ref, sems, w_ref, p_ref = refs[chunks + 2 :]
-    fold = lax.axis_size("col") // lax.axis_size("row")
-    col = lax.axis_index("col")
-    place_ref[0] = jnp.bitwise_xor(lax.div(col, fold), lax.axis_index("row")).astype(jnp.int32)
-    place_ref[1] = lax.rem(col, fold).astype(jnp.int32)
+def project_kernel(seqs, residues, width, chunks, shift_ref, member_ref, x_hbm, gain_hbm, bias_hbm, lw_hbm, rw_hbm, *refs):
+    left_refs, right_ref = refs[:chunks], refs[chunks]
+    x_ref, gain_ref, bias_ref, lw_ref, rw_ref, sems, w_ref, p_ref = refs[chunks + 1 :]
     channels = x_ref.shape[1]
     per = LANES // width
     groups = residues // per
@@ -90,7 +86,7 @@
                     left_refs[g // share][to, at * LANES : (at + 1) * LANES] = value
 
 
-def project(alignment, gain, bias, left_weight, right_weight, chunks):
+def project(place, alignment, gain, bias, left_weight, right_weight, chunks):
     seq_local, residues, channels = alignment.shape
     width = left_weight.shape[1]
     steps = 4
@@ -98,13 +94,12 @@
     span = residues * width
     outs = [jax.ShapeDtypeStruct((seq_local, span // chunks), F32)] * chunks + [
         jax.ShapeDtypeStruct((seq_local, span), F32),
-        jax.ShapeDtypeStruct((2,), jnp.int32),
     ]
     return pl.pallas_call(
         functools.partial(project_kernel, seqs, residues, width, chunks),
         out_shape=outs,
-        in_specs=[pl.BlockSpec(memory_space=pltpu.HBM)] * 5,
-        out_specs=[pl.BlockSpec(memory_space=pltpu.VMEM)] * (len(outs) - 1) + [pl.BlockSpec(memory_space=pltpu.SMEM)],
+        in_specs=[pl.BlockSpec(memory_space=pltpu.SMEM)] * 2 + [pl.BlockSpec(memory_space=pltpu.HBM)] * 5,
+        out_specs=[pl.BlockSpec(memory_space=pltpu.VMEM)] * len(outs),
         scratch_shapes=[
             pltpu.VMEM((seq_local * residues, channels), F32),
             pltpu.VMEM((1, channels), F32),
@@ -119,6 +114,7 @@
         compiler_params=pltpu.CompilerParams(vmem_limit_bytes=VMEM),
         name="project",
     )(
+        *place,
         *(
             pltpu.with_memory_space_constraint(a, pltpu.HBM)
             for a in (
@@ -198,12 +194,7 @@
         @pl.when(t_ref[0] == t)
         def _():
             for m in range(slots):
-                at = m ^ t
-                value = ins[at][...]
-                if at == slots - 1:
-                    for extra in ins[slots:]:
-                        value = value + extra[...]
-                outs[m][...] = value
+                outs[m][...] = ins[m ^ t][...]
 
 
 def route(t, slots, ins):
@@ -290,9 +281,9 @@
     tiles = residues // tile
 
     def tile_at(s, place):
-        member = jnp.bitwise_xor(place[1], members[0])
+        member = jnp.bitwise_xor(place[0], members[0])
         for n in range(1, len(members)):
-            member = jnp.where(s >= n * steps, jnp.bitwise_xor(place[1], members[n]), member)
+            member = jnp.where(s >= n * steps, jnp.bitwise_xor(place[0], members[n]), member)
         return member * tiles + chunk * steps + lax.rem(s, steps), 0, 0
 
     rows = pl.BlockSpec((tile, residues, pair), tile_at)
@@ -360,16 +351,13 @@
     def along_members(value, n):
         return lax.ppermute(value, "col", [(a, a ^ n) for a in range(cols)])
 
-    *lefts, right, place = project(alignment, align_gain, align_bias, left_weight, right_weight, chunks)
+    col = lax.axis_index("col")
+    shift = jnp.bitwise_xor(lax.div(col, fold), lax.axis_index("row")).astype(jnp.int32).reshape(1)
+    member = lax.rem(col, fold).astype(jnp.int32).reshape(1)
+    *lefts, right = project((shift, member), alignment, align_gain, align_bias, left_weight, right_weight, chunks)
 
     def spread(left):
-        if rows != 4:
-            return [left] + [along_groups(left, [(a, a ^ m) for a in range(rows)]) for m in range(1, rows)]
-        two = along_groups(left, [(a, a ^ 2) for a in range(4)])
-        one = along_groups(left, [(a, a ^ 1) for a in range(4)])
-        three = along_groups(left, [(1, 2), (2, 1)])
-        relayed = along_groups(two, [(1, 0), (2, 3)])
-        return [left, one, two, three, relayed]
+        return [left] + [along_groups(left, [(a, a ^ m) for a in range(rows)]) for m in range(1, rows)]
 
     slots = [spread(left) for left in lefts]
     rights = [right] + [along_rows(right, m) for m in range(1, rows)]
@@ -379,15 +367,12 @@
 
     out = None
     for chunk in range(chunks):
-        routed = route(place, rows, slots[chunk])
+        routed = route(shift, rows, slots[chunk])
         mine = [routed[0]] + [along_rows(routed[m], m) for m in range(1, rows)]
         packed = pack(mine)
         blocks = [packed] + [along_members(packed, n) for n in range(1, fold)]
-        calls = [[n] for n in range(fold)] if chunk == chunks - 1 else [list(range(fold))]
-        for members in calls:
-            out = pair_update(
-                place, members, chunk, [blocks[n] for n in members], rt, weights, vectors, pair_state, out, width
-            )
+        for n in range(fold):
+            out = pair_update(member, [n], chunk, [blocks[n]], rt, weights, vectors, pair_state, out, width)
     return out
 
 

time: 67.8 us -> 66.4 us (0.979)
  the two profiles are of different devices: /device:TPU:0 before, /device:TPU:17 now
where the time goes in v2:
time: 66.4 us; the launch traced here: 66.2 us
  waiting for transfers between devices  26.6 us (40%)
  starting transfers between devices  21.2 us (32%)
  Pallas kernels  18 us (27%)
    ppermute x6, waiting for transfers between devices, along_groups(): lax.ppermute(value, 'col', [(a * fold + k, b * fold + k) for a, b in pair...  16.5 us
    pallas_call x4, Pallas kernels, pair_update(): pl.pallas_call(functools.partial(pair_kernel, len(lefts), steps, tile, wi...  12.9 us
    ppermute x9, waiting for transfers between devices, along_rows(): return lax.ppermute(value, 'row', [(a, a ^ m) for a in range(rows)])  10.2 us
    ppermute x9, starting transfers between devices, along_rows(): return lax.ppermute(value, 'row', [(a, a ^ m) for a in range(rows)])  8.93 us
    ppermute x2, starting transfers between devices, along_members(): return lax.ppermute(value, 'col', [(a, a ^ n) for a in range(cols)])  6.16 us
    ppermute x6, starting transfers between devices, along_groups(): lax.ppermute(value, 'col', [(a * fold + k, b * fold + k) for a, b in pair...  6.1 us
    pallas_call x1, Pallas kernels, project(): pl.pallas_call(functools.partial(project_kernel, seqs, residues, width, c...  3.37 us
  transfers between devices with their start and end apart: 17, of which 4 were waited for; matrix products, arithmetic and copies ran while one was open for 0% of the time, Pallas kernels for 17%

profile of v2, /device:TPU:17, one launch (start us, length us, event | category | flops | bytes accessed | tf_op | source)
XLA Modules:
  0.0 66.2 jit_solution(18066686117327822185)
XLA Ops:
  0.0 3.4 %project.1 = (f32[64,512]{1,0:T(8,128)S(1)}, f32[64,512]{1,0:T(8,128)S(1)}, f32[64,1024]{1,0:T(8,128)S(1)}) custom-call(s32[1]{0:T(128)} %bitcast.1.shift_ref.t_ref, s32[1]{0:T(128)} %bitcast.member_ref.at_ref, f32[2048,256]{1,0:T(8,128)} %bitcast.32, f32[1,256]{1,0:T(1,128)} %bitcast.35, f32[1,256]{1,0:T(1,128)} %bitcast.36, f32[32,256]{1,0:T(8,128)} %bitcast.33, ...), custom_call_target="tpu_custom_call" | custom-call | flops 6000000000 | bytes 4000000 | tf_op jit(solution)/shard_map/project/pallas_call | solution.py:98
  3.4 0.0 copy-start.6
  3.4 0.0 copy-start.7
  3.4 0.0 copy-start.8
  3.4 1.4 %collective-permute-start.10 = (f32[64,512]{1,0:T(8,128)S(1)}, f32[64,512]{1,0:T(8,128)S(1)}, u32[]{:S(2)}, u32[]{:S(2)}) collective-permute-start(f32[64,512]{1,0:T(8,128)S(1)} %get-tuple-element.28.refs_0_), channel_id=1, source_target_pairs={{0,2},{1,3},{2,0},{3,1},{4,6},{5,7},{6,4},{7,5},{8,10},{9,11},{10,... | collective-permute-start | bytes 393224 | tf_op jit(solution)/shard_map/ppermute | solution.py:346
  4.8 0.1 collective-permute-start.11
  4.8 1.3 %collective-permute-start.12 = (f32[64,512]{1,0:T(8,128)S(1)}, f32[64,512]{1,0:T(8,128)S(1)}, u32[]{:S(2)}, u32[]{:S(2)}) collective-permute-start(f32[64,512]{1,0:T(8,128)S(1)} %get-tuple-element.28.refs_0_), channel_id=1, source_target_pairs={{0,6},{1,7},{2,4},{3,5},{4,2},{5,3},{6,0},{7,1},{8,14},{9,15},{10,... | collective-permute-start | bytes 393224 | tf_op jit(solution)/shard_map/ppermute | solution.py:346
  6.1 2.2 %collective-permute-start = (f32[64,512]{1,0:T(8,128)S(1)}, f32[64,512]{1,0:T(8,128)S(1)}, u32[]{:S(2)}, u32[]{:S(2)}) collective-permute-start(f32[64,512]{1,0:T(8,128)S(1)} %get-tuple-element.19.refs_0_), channel_id=1, source_target_pairs={{0,2},{1,3},{2,0},{3,1},{4,6},{5,7},{6,4},{7,5},{8,10},{9,11},{10,... | collective-permute-start | bytes 393224 | tf_op jit(solution)/shard_map/ppermute | solution.py:346
  8.3 0.0 collective-permute-start.1
  8.3 0.0 collective-permute-done.10.refs_1_
  8.3 1.2 %collective-permute-start.2 = (f32[64,512]{1,0:T(8,128)S(1)}, f32[64,512]{1,0:T(8,128)S(1)}, u32[]{:S(2)}, u32[]{:S(2)}) collective-permute-start(f32[64,512]{1,0:T(8,128)S(1)} %get-tuple-element.19.refs_0_), channel_id=1, source_target_pairs={{0,6},{1,7},{2,4},{3,5},{4,2},{5,3},{6,0},{7,1},{8,14},{9,15},{10,... | collective-permute-start | bytes 393224 | tf_op jit(solution)/shard_map/ppermute | solution.py:346
  9.5 1.3 %collective-permute-done.11.refs_2_ = f32[64,512]{1,0:T(8,128)S(1)} collective-permute-done((f32[64,512]{1,0:T(8,128)S(1)}, f32[64,512]{1,0:T(8,128)S(1)}, u32[]{:S(2)}, u32[]{:S(2)}) %collective-permute-start.11) | collective-permute-done | bytes 131104 | tf_op jit(solution)/shard_map/ppermute | solution.py:346
  10.8 12.3 %collective-permute-done.12.refs_3_ = f32[64,512]{1,0:T(8,128)S(1)} collective-permute-done((f32[64,512]{1,0:T(8,128)S(1)}, f32[64,512]{1,0:T(8,128)S(1)}, u32[]{:S(2)}, u32[]{:S(2)}) %collective-permute-start.12) | collective-permute-done | bytes 131104 | tf_op jit(solution)/shard_map/ppermute | solution.py:346
  23.2 1.3 %collective-permute-start.13 = (f32[64,512]{1,0:T(8,128)S(1)}, f32[64,512]{1,0:T(8,128)S(1)}, u32[]{:S(2)}, u32[]{:S(2)}) collective-permute-start(f32[64,512]{1,0:T(8,128)S(1)} %get-tuple-element.30), channel_id=1, source_target_pairs={{0,8},{8,0},{16,24},{24,16},{1,9},{9,1},{17,25},{25,17},{2,10},{10... | collective-permute-start | bytes 393224 | tf_op jit(solution)/shard_map/ppermute | solution.py:349
  24.4 1.3 %collective-permute-start.14 = (f32[64,512]{1,0:T(8,128)S(1)}, f32[64,512]{1,0:T(8,128)S(1)}, u32[]{:S(2)}, u32[]{:S(2)}) collective-permute-start(f32[64,512]{1,0:T(8,128)S(1)} %get-tuple-element.31), channel_id=1, source_target_pairs={{0,16},{8,24},{16,0},{24,8},{1,17},{9,25},{17,1},{25,9},{2,18},{10... | collective-permute-start | bytes 393224 | tf_op jit(solution)/shard_map/ppermute | solution.py:349
  25.7 0.0 collective-permute-done.refs_1_
  25.7 0.2 collective-permute-start.15
  25.9 0.0 collective-permute-done.1.refs_2_
  25.9 2.8 %collective-permute-done.2.refs_3_ = f32[64,512]{1,0:T(8,128)S(1)} collective-permute-done((f32[64,512]{1,0:T(8,128)S(1)}, f32[64,512]{1,0:T(8,128)S(1)}, u32[]{:S(2)}, u32[]{:S(2)}) %collective-permute-start.2) | collective-permute-done | bytes 131104 | tf_op jit(solution)/shard_map/ppermute | solution.py:346
  28.8 0.2 route.2
  29.0 1.3 %collective-permute-start.3 = (f32[64,512]{1,0:T(8,128)S(1)}, f32[64,512]{1,0:T(8,128)S(1)}, u32[]{:S(2)}, u32[]{:S(2)}) collective-permute-start(f32[64,512]{1,0:T(8,128)S(1)} %get-tuple-element.21), channel_id=1, source_target_pairs={{0,8},{8,0},{16,24},{24,16},{1,9},{9,1},{17,25},{25,17},{2,10},{10... | collective-permute-start | bytes 393224 | tf_op jit(solution)/shard_map/ppermute | solution.py:349
  30.2 1.3 %collective-permute-start.4 = (f32[64,512]{1,0:T(8,128)S(1)}, f32[64,512]{1,0:T(8,128)S(1)}, u32[]{:S(2)}, u32[]{:S(2)}) collective-permute-start(f32[64,512]{1,0:T(8,128)S(1)} %get-tuple-element.22), channel_id=1, source_target_pairs={{0,16},{8,24},{16,0},{24,8},{1,17},{9,25},{17,1},{25,9},{2,18},{10... | collective-permute-start | bytes 393224 | tf_op jit(solution)/shard_map/ppermute | solution.py:349
  31.5 0.0 collective-permute-done.13.refs_1_
  31.5 0.3 collective-permute-start.7
  31.8 0.0 collective-permute-done.14.refs_2_
  31.8 0.2 collective-permute-start.8
  32.0 0.0 collective-permute-done.15.refs_3_
  32.0 2.2 %collective-permute-start.9 = (f32[64,1024]{1,0:T(8,128)S(1)}, f32[64,1024]{1,0:T(8,128)S(1)}, u32[]{:S(2)}, u32[]{:S(2)}) collective-permute-start(f32[64,1024]{1,0:T(8,128)S(1)} %get-tuple-element.24.refs_0_), channel_id=1, source_target_pairs={{0,24},{8,16},{16,8},{24,0},{1,25},{9,17},{17,9},{25,1},{2,26},{10... | collective-permute-start | bytes 786440 | tf_op jit(solution)/shard_map/ppermute | solution.py:349
  34.2 0.0 collective-permute-done.3.refs_1_
  34.2 3.9 %collective-permute-start.16 = (f32[256,512]{1,0:T(8,128)S(1)}, f32[256,512]{1,0:T(8,128)S(1)}, u32[]{:S(2)}, u32[]{:S(2)}) collective-permute-start(f32[256,512]{1,0:T(8,128)S(1)} %pack.3.refs_0_), channel_id=1, source_target_pairs={{0,1},{1,0},{2,3},{3,2},{4,5},{5,4},{6,7},{7,6},{8,9},{9,8},{10,11... | collective-permute-start | bytes 1572872 | tf_op jit(solution)/shard_map/ppermute | solution.py:352
  38.1 0.0 collective-permute-done.4.refs_2_
  38.1 1.0 %collective-permute-start.5 = (f32[64,512]{1,0:T(8,128)S(1)}, f32[64,512]{1,0:T(8,128)S(1)}, u32[]{:S(2)}, u32[]{:S(2)}) collective-permute-start(f32[64,512]{1,0:T(8,128)S(1)} %get-tuple-element.23), channel_id=1, source_target_pairs={{0,24},{8,16},{16,8},{24,0},{1,25},{9,17},{17,9},{25,1},{2,26},{10... | collective-permute-start | bytes 393224 | tf_op jit(solution)/shard_map/ppermute | solution.py:349
  39.2 10.1 %collective-permute-done.5.refs_3_ = f32[64,512]{1,0:T(8,128)S(1)} collective-permute-done((f32[64,512]{1,0:T(8,128)S(1)}, f32[64,512]{1,0:T(8,128)S(1)}, u32[]{:S(2)}, u32[]{:S(2)}) %collective-permute-start.5) | collective-permute-done | bytes 131104 | tf_op jit(solution)/shard_map/ppermute | solution.py:349
  49.3 2.3 %collective-permute-start.6 = (f32[256,512]{1,0:T(8,128)S(1)}, f32[256,512]{1,0:T(8,128)S(1)}, u32[]{:S(2)}, u32[]{:S(2)}) collective-permute-start(f32[256,512]{1,0:T(8,128)S(1)} %pack.2.refs_0_), channel_id=1, source_target_pairs={{0,1},{1,0},{2,3},{3,2},{4,5},{5,4},{6,7},{7,6},{8,9},{9,8},{10,11... | collective-permute-start | bytes 1572872 | tf_op jit(solution)/shard_map/ppermute | solution.py:352
  51.6 0.0 copy-done.6
  51.6 0.0 copy-done.7
  51.6 0.0 copy-done.8
  51.6 0.4 weights.1
  52.1 0.0 copy-start
  52.1 0.0 copy-start.1
  52.1 0.0 copy-start.2
  52.1 0.0 copy-start.3
  52.1 0.0 copy-start.4
  52.1 0.0 copy-start.5
  52.1 0.0 collective-permute-done.7.refs_1_
  52.1 0.0 collective-permute-done.8.refs_2_
  52.1 0.0 collective-permute-done.9.refs_3_
  52.2 1.0 %turn.1.refs_1_ = bf16[1024,768]{1,0:T(8,128)(2,1)S(1)} custom-call(f32[64,1024]{1,0:T(8,128)S(1)} %get-tuple-element.24.refs_0_, f32[64,1024]{1,0:T(8,128)S(1)} %collective-permute-done.7.refs_1_, f32[64,1024]{1,0:T(8,128)S(1)} %collective-permute-done.8.refs_2_, f32[64,1024]{1,0:T(8,128)S(1)} %collective-permute-done.9.refs_3_), custom_call_target="tpu_custom_call" | custom-call | flops 2000000000 | bytes 3000000 | tf_op jit(solution)/shard_map/turn/pallas_call | solution.py:180
  53.1 0.2 copy-done
  53.3 0.0 copy-done.1
  53.3 0.0 copy-done.2
  53.3 0.0 copy-done.3
  53.3 0.0 copy-done.4
  53.3 0.0 copy-done.5
  53.3 3.2 %pair.4.refs_11_ = f32[64,32,128]{2,1,0:T(8,128)} custom-call(s32[1]{0:T(128)} %bitcast.member_ref.at_ref, f32[256,512]{1,0:T(8,128)S(1)} %pack.3.refs_0_, bf16[1024,768]{1,0:T(8,128)(2,1)S(1)} %turn.1.refs_1_, bf16[1024,256]{1,0:T(8,128)(2,1)S(1)} %get-tuple-element.25.refs_2_, bf16[384,512]{1,0:T(8,128)(2,1)S(1)} %get-tuple-element.26.refs_3_, ...), custom_call_target="tpu_custom_call" | custom-call | flops 1000000000 | bytes 4000000 | tf_op jit(solution)/shard_map/pair/pallas_call | solution.py:302
  56.5 0.0 collective-permute-done.16.refs_0_
  56.5 3.2 %pair.5.refs_11_ = f32[64,32,128]{2,1,0:T(8,128)} custom-call(s32[1]{0:T(128)} %bitcast.member_ref.at_ref, f32[256,512]{1,0:T(8,128)S(1)} %collective-permute-done.16.refs_0_, bf16[1024,768]{1,0:T(8,128)(2,1)S(1)} %turn.1.refs_1_, bf16[1024,256]{1,0:T(8,128)(2,1)S(1)} %get-tuple-element.25.refs_2_, ...), custom_call_target="tpu_custom_call", output_to_operand_aliasing={{}: (12, {})} | custom-call | flops 1000000000 | bytes 4000000 | tf_op jit(solution)/shard_map/pair/pallas_call | solution.py:302
  59.8 3.2 %pair.6.refs_11_ = f32[64,32,128]{2,1,0:T(8,128)} custom-call(s32[1]{0:T(128)} %bitcast.member_ref.at_ref, f32[256,512]{1,0:T(8,128)S(1)} %pack.2.refs_0_, bf16[1024,768]{1,0:T(8,128)(2,1)S(1)} %turn.1.refs_1_, bf16[1024,256]{1,0:T(8,128)(2,1)S(1)} %get-tuple-element.25.refs_2_, ...), custom_call_target="tpu_custom_call", output_to_operand_aliasing={{}: (12, {})} | custom-call | flops 1000000000 | bytes 4000000 | tf_op jit(solution)/shard_map/pair/pallas_call | solution.py:302
  63.0 0.0 collective-permute-done.6.refs_0_
  63.0 3.2 %pair.7 = f32[64,32,128]{2,1,0:T(8,128)} custom-call(s32[1]{0:T(128)} %bitcast.member_ref.at_ref, f32[256,512]{1,0:T(8,128)S(1)} %collective-permute-done.6.refs_0_, bf16[1024,768]{1,0:T(8,128)(2,1)S(1)} %turn.1.refs_1_, bf16[1024,256]{1,0:T(8,128)(2,1)S(1)} %get-tuple-element.25.refs_2_, ...), custom_call_target="tpu_custom_call", output_to_operand_aliasing={{}: (12, {})} | custom-call | flops 1000000000 | bytes 4000000 | tf_op jit(solution)/shard_map/pair/pallas_call | solution.py:302
  (3 shorter events, 0.1 us)
Async XLA Ops:
  3.4 48.2 %copy-start.6 = (f32[1024,128]{1,0:T(8,128)S(1)}, f32[1024,128]{1,0:T(8,128)}, u32[]{:S(2)}) copy-start(f32[1024,128]{1,0:T(8,128)} %wp_ref.1) | copy-start | bytes 1572868
  3.4 48.2 %copy-start.7 = (f32[128,512]{1,0:T(8,128)S(1)}, f32[128,512]{1,0:T(8,128)}, u32[]{:S(2)}) copy-start(f32[128,512]{1,0:T(8,128)} %wh_ref.1) | copy-start | bytes 786436
  3.4 48.2 %copy-start.8 = (f32[512,128]{1,0:T(8,128)S(1)}, f32[512,128]{1,0:T(8,128)}, u32[]{:S(2)}) copy-start(f32[512,128]{1,0:T(8,128)} %wf_ref.1) | copy-start | bytes 786436
  3.4 4.9 %collective-permute-start.10 = (f32[64,512]{1,0:T(8,128)S(1)}, f32[64,512]{1,0:T(8,128)S(1)}, u32[]{:S(2)}, u32[]{:S(2)}) collective-permute-start(f32[64,512]{1,0:T(8,128)S(1)} %get-tuple-element.28.refs_0_), channel_id=1, source_target_pairs={{0,2},{1,3},{2,0},{3,1},{4,6},{5,7},{6,4},{7,5},{8,10},{9,11},{10,... | collective-permute-start | bytes 393224 | tf_op jit(solution)/shard_map/ppermute | solution.py:346
  4.8 6.0 %collective-permute-start.11 = (f32[64,512]{1,0:T(8,128)S(1)}, f32[64,512]{1,0:T(8,128)S(1)}, u32[]{:S(2)}, u32[]{:S(2)}) collective-permute-start(f32[64,512]{1,0:T(8,128)S(1)} %get-tuple-element.28.refs_0_), channel_id=1, source_target_pairs={{0,4},{1,5},{2,6},{3,7},{4,0},{5,1},{6,2},{7,3},{8,12},{9,13},{10,... | collective-permute-start | bytes 393224 | tf_op jit(solution)/shard_map/ppermute | solution.py:346
  4.8 18.3 %collective-permute-start.12 = (f32[64,512]{1,0:T(8,128)S(1)}, f32[64,512]{1,0:T(8,128)S(1)}, u32[]{:S(2)}, u32[]{:S(2)}) collective-permute-start(f32[64,512]{1,0:T(8,128)S(1)} %get-tuple-element.28.refs_0_), channel_id=1, source_target_pairs={{0,6},{1,7},{2,4},{3,5},{4,2},{5,3},{6,0},{7,1},{8,14},{9,15},{10,... | collective-permute-start | bytes 393224 | tf_op jit(solution)/shard_map/ppermute | solution.py:346
  6.1 19.6 %collective-permute-start = (f32[64,512]{1,0:T(8,128)S(1)}, f32[64,512]{1,0:T(8,128)S(1)}, u32[]{:S(2)}, u32[]{:S(2)}) collective-permute-start(f32[64,512]{1,0:T(8,128)S(1)} %get-tuple-element.19.refs_0_), channel_id=1, source_target_pairs={{0,2},{1,3},{2,0},{3,1},{4,6},{5,7},{6,4},{7,5},{8,10},{9,11},{10,... | collective-permute-start | bytes 393224 | tf_op jit(solution)/shard_map/ppermute | solution.py:346
  8.3 17.6 %collective-permute-start.1 = (f32[64,512]{1,0:T(8,128)S(1)}, f32[64,512]{1,0:T(8,128)S(1)}, u32[]{:S(2)}, u32[]{:S(2)}) collective-permute-start(f32[64,512]{1,0:T(8,128)S(1)} %get-tuple-element.19.refs_0_), channel_id=1, source_target_pairs={{0,4},{1,5},{2,6},{3,7},{4,0},{5,1},{6,2},{7,3},{8,12},{9,13},{10,... | collective-permute-start | bytes 393224 | tf_op jit(solution)/shard_map/ppermute | solution.py:346
  8.3 20.4 %collective-permute-start.2 = (f32[64,512]{1,0:T(8,128)S(1)}, f32[64,512]{1,0:T(8,128)S(1)}, u32[]{:S(2)}, u32[]{:S(2)}) collective-permute-start(f32[64,512]{1,0:T(8,128)S(1)} %get-tuple-element.19.refs_0_), channel_id=1, source_target_pairs={{0,6},{1,7},{2,4},{3,5},{4,2},{5,3},{6,0},{7,1},{8,14},{9,15},{10,... | collective-permute-start | bytes 393224 | tf_op jit(solution)/shard_map/ppermute | solution.py:346
  23.2 8.3 %collective-permute-start.13 = (f32[64,512]{1,0:T(8,128)S(1)}, f32[64,512]{1,0:T(8,128)S(1)}, u32[]{:S(2)}, u32[]{:S(2)}) collective-permute-start(f32[64,512]{1,0:T(8,128)S(1)} %get-tuple-element.30), channel_id=1, source_target_pairs={{0,8},{8,0},{16,24},{24,16},{1,9},{9,1},{17,25},{25,17},{2,10},{10... | collective-permute-start | bytes 393224 | tf_op jit(solution)/shard_map/ppermute | solution.py:349
  24.4 7.3 %collective-permute-start.14 = (f32[64,512]{1,0:T(8,128)S(1)}, f32[64,512]{1,0:T(8,128)S(1)}, u32[]{:S(2)}, u32[]{:S(2)}) collective-permute-start(f32[64,512]{1,0:T(8,128)S(1)} %get-tuple-element.31), channel_id=1, source_target_pairs={{0,16},{8,24},{16,0},{24,8},{1,17},{9,25},{17,1},{25,9},{2,18},{10... | collective-permute-start | bytes 393224 | tf_op jit(solution)/shard_map/ppermute | solution.py:349
  25.7 6.3 %collective-permute-start.15 = (f32[64,512]{1,0:T(8,128)S(1)}, f32[64,512]{1,0:T(8,128)S(1)}, u32[]{:S(2)}, u32[]{:S(2)}) collective-permute-start(f32[64,512]{1,0:T(8,128)S(1)} %get-tuple-element.32), channel_id=1, source_target_pairs={{0,24},{8,16},{16,8},{24,0},{1,25},{9,17},{17,9},{25,1},{2,26},{10... | collective-permute-start | bytes 393224 | tf_op jit(solution)/shard_map/ppermute | solution.py:349
  29.0 5.2 %collective-permute-start.3 = (f32[64,512]{1,0:T(8,128)S(1)}, f32[64,512]{1,0:T(8,128)S(1)}, u32[]{:S(2)}, u32[]{:S(2)}) collective-permute-start(f32[64,512]{1,0:T(8,128)S(1)} %get-tuple-element.21), channel_id=1, source_target_pairs={{0,8},{8,0},{16,24},{24,16},{1,9},{9,1},{17,25},{25,17},{2,10},{10... | collective-permute-start | bytes 393224 | tf_op jit(solution)/shard_map/ppermute | solution.py:349
  30.2 7.9 %collective-permute-start.4 = (f32[64,512]{1,0:T(8,128)S(1)}, f32[64,512]{1,0:T(8,128)S(1)}, u32[]{:S(2)}, u32[]{:S(2)}) collective-permute-start(f32[64,512]{1,0:T(8,128)S(1)} %get-tuple-element.22), channel_id=1, source_target_pairs={{0,16},{8,24},{16,0},{24,8},{1,17},{9,25},{17,1},{25,9},{2,18},{10... | collective-permute-start | bytes 393224 | tf_op jit(solution)/shard_map/ppermute | solution.py:349
  31.5 20.6 %collective-permute-start.7 = (f32[64,1024]{1,0:T(8,128)S(1)}, f32[64,1024]{1,0:T(8,128)S(1)}, u32[]{:S(2)}, u32[]{:S(2)}) collective-permute-start(f32[64,1024]{1,0:T(8,128)S(1)} %get-tuple-element.24.refs_0_), channel_id=1, source_target_pairs={{0,8},{8,0},{16,24},{24,16},{1,9},{9,1},{17,25},{25,17},{2,10},{10... | collective-permute-start | bytes 786440 | tf_op jit(solution)/shard_map/ppermute | solution.py:349
  31.8 20.4 %collective-permute-start.8 = (f32[64,1024]{1,0:T(8,128)S(1)}, f32[64,1024]{1,0:T(8,128)S(1)}, u32[]{:S(2)}, u32[]{:S(2)}) collective-permute-start(f32[64,1024]{1,0:T(8,128)S(1)} %get-tuple-element.24.refs_0_), channel_id=1, source_target_pairs={{0,16},{8,24},{16,0},{24,8},{1,17},{9,25},{17,1},{25,9},{2,18},{10... | collective-permute-start | bytes 786440 | tf_op jit(solution)/shard_map/ppermute | solution.py:349
  32.0 20.2 %collective-permute-start.9 = (f32[64,1024]{1,0:T(8,128)S(1)}, f32[64,1024]{1,0:T(8,128)S(1)}, u32[]{:S(2)}, u32[]{:S(2)}) collective-permute-start(f32[64,1024]{1,0:T(8,128)S(1)} %get-tuple-element.24.refs_0_), channel_id=1, source_target_pairs={{0,24},{8,16},{16,8},{24,0},{1,25},{9,17},{17,9},{25,1},{2,26},{10... | collective-permute-start | bytes 786440 | tf_op jit(solution)/shard_map/ppermute | solution.py:349
  34.2 22.3 %collective-permute-start.16 = (f32[256,512]{1,0:T(8,128)S(1)}, f32[256,512]{1,0:T(8,128)S(1)}, u32[]{:S(2)}, u32[]{:S(2)}) collective-permute-start(f32[256,512]{1,0:T(8,128)S(1)} %pack.3.refs_0_), channel_id=1, source_target_pairs={{0,1},{1,0},{2,3},{3,2},{4,5},{5,4},{6,7},{7,6},{8,9},{9,8},{10,11... | collective-permute-start | bytes 1572872 | tf_op jit(solution)/shard_map/ppermute | solution.py:352
  38.1 11.2 %collective-permute-start.5 = (f32[64,512]{1,0:T(8,128)S(1)}, f32[64,512]{1,0:T(8,128)S(1)}, u32[]{:S(2)}, u32[]{:S(2)}) collective-permute-start(f32[64,512]{1,0:T(8,128)S(1)} %get-tuple-element.23), channel_id=1, source_target_pairs={{0,24},{8,16},{16,8},{24,0},{1,25},{9,17},{17,9},{25,1},{2,26},{10... | collective-permute-start | bytes 393224 | tf_op jit(solution)/shard_map/ppermute | solution.py:349
  49.3 13.6 %collective-permute-start.6 = (f32[256,512]{1,0:T(8,128)S(1)}, f32[256,512]{1,0:T(8,128)S(1)}, u32[]{:S(2)}, u32[]{:S(2)}) collective-permute-start(f32[256,512]{1,0:T(8,128)S(1)} %pack.2.refs_0_), channel_id=1, source_target_pairs={{0,1},{1,0},{2,3},{3,2},{4,5},{5,4},{6,7},{7,6},{8,9},{9,8},{10,11... | collective-permute-start | bytes 1572872 | tf_op jit(solution)/shard_map/ppermute | solution.py:352
  52.1 1.2 %copy-start = (f32[64,32,128]{2,1,0:T(8,128)S(1)}, f32[64,32,128]{2,1,0:T(8,128)}, u32[]{:S(2)}) copy-start(f32[64,32,128]{2,1,0:T(8,128)} %refs_10_.7) | copy-start | bytes 3145732
  52.1 1.2 %copy-start.1 = (f32[512]{0:T(512)S(1)}, f32[512]{0:T(512)}, u32[]{:S(2)}) copy-start(f32[512]{0:T(512)} %param.25) | copy-start | bytes 6148
  52.1 1.2 %copy-start.2 = (f32[128]{0:T(128)S(1)}, f32[128]{0:T(128)}, u32[]{:S(2)}) copy-start(f32[128]{0:T(128)} %param.20) | copy-start | bytes 1540
  52.1 1.2 %copy-start.3 = (f32[128]{0:T(128)S(1)}, f32[128]{0:T(128)}, u32[]{:S(2)}) copy-start(f32[128]{0:T(128)} %param.22) | copy-start | bytes 1540
  52.1 1.2 %copy-start.4 = (f32[128]{0:T(128)S(1)}, f32[128]{0:T(128)}, u32[]{:S(2)}) copy-start(f32[128]{0:T(128)} %param.23) | copy-start | bytes 1540
  52.1 1.2 %copy-start.5 = (f32[128]{0:T(128)S(1)}, f32[128]{0:T(128)}, u32[]{:S(2)}) copy-start(f32[128]{0:T(128)} %param.27) | copy-start | bytes 1540

commit v3 on v2

--- a/solution.py
+++ b/solution.py
@@ -32,100 +32,117 @@
     return centred * lax.rsqrt(spread + EPS) * gain + offset
 
 
-def project_kernel(seqs, residues, width, chunks, shift_ref, member_ref, x_hbm, gain_hbm, bias_hbm, lw_hbm, rw_hbm, *refs):
-    left_refs, right_ref = refs[:chunks], refs[chunks]
-    x_ref, gain_ref, bias_ref, lw_ref, rw_ref, sems, w_ref, p_ref = refs[chunks + 1 :]
-    channels = x_ref.shape[1]
+def project_kernel(chunk, steps, width, shift_ref, member_ref, x_hbm, *refs):
+    if chunk:
+        w_ref, offset_ref, before_ref, left_ref, right_ref, p_ref = refs
+        x_ref = x_hbm
+    else:
+        gain_hbm, bias_hbm, lw_hbm, rw_hbm, *refs = refs
+        left_ref, right_ref, w_ref, offset_ref, rest_ref, p_ref, x_ref, sems, gain_ref, bias_ref, lw_ref, rw_ref = refs
+        small = ((lw_hbm, lw_ref), (rw_hbm, rw_ref), (gain_hbm, gain_ref), (bias_hbm, bias_ref))
+    seq_local, residues, channels = x_ref.shape
+    seqs = seq_local // steps
     per = LANES // width
     groups = residues // per
-    block = seqs * residues
-    steps = x_ref.shape[0] // block
-
-    small = ((lw_hbm, lw_ref), (rw_hbm, rw_ref), (gain_hbm, gain_ref), (bias_hbm, bias_ref))
-    copies = [pltpu.make_async_copy(a, b, sems.at[n]) for n, (a, b) in enumerate(small)]
-    for step in range(steps):
-        rows = pl.ds(step * block, block)
-        copies.append(pltpu.make_async_copy(x_hbm.at[rows], x_ref.at[rows], sems.at[len(small) + step]))
-    for copy in copies:
-        copy.start()
-    for copy in copies[: len(small)]:
-        copy.wait()
-    plain = jnp.concatenate([lw_ref[...], rw_ref[...]], axis=0)
-    high, low = split(jnp.concatenate([plain * gain_ref[...], plain], axis=0).T)
-    w_ref[:, :LANES] = high
-    w_ref[:, LANES:] = low
+
+    if not chunk:
+        copies = [pltpu.make_async_copy(a, b, sems.at[steps + n]) for n, (a, b) in enumerate(small)]
+        blocks = []
+        for step in range(steps):
+            rows = pl.ds(step * seqs, seqs)
+            blocks.append(
+                pltpu.make_async_copy(x_hbm.at[rows, pl.ds(0, residues)], x_ref.at[rows], sems.at[step])
+            )
+        rest = x_hbm.at[:, pl.ds(residues, rest_ref.shape[1])]
+        rest = pltpu.make_async_copy(rest, rest_ref, sems.at[steps + len(small)])
+        for copy in copies + blocks + [rest]:
+            copy.start()
+        for copy in copies:
+            copy.wait()
 
     def multiply(values):
         high, low = split(values)
         both = dot(high, w_ref[...])
         return both[:, :LANES] + both[:, LANES:] + dot(low, w_ref[:, :LANES])
 
-    offset = multiply(jnp.broadcast_to(bias_ref[...], (8, channels)))
-    offset = pltpu.roll(offset, LANES - 2 * width, 1)[:1]
+    if chunk:
+        right_ref[:, : chunk * residues * width] = before_ref[...]
+    else:
+        plain = jnp.concatenate([lw_ref[...], rw_ref[...]], axis=0)
+        high, low = split(jnp.concatenate([plain * gain_ref[...], plain], axis=0).T)
+        w_ref[:, :LANES] = high
+        w_ref[:, LANES:] = low
+        offset_ref[...] = pltpu.roll(multiply(jnp.broadcast_to(bias_ref[...], (8, channels))), LANES - 2 * width, 1)
+    offset = offset_ref[:1]
     lane = lax.broadcasted_iota(jnp.int32, (seqs, LANES), 1) // width
-    share = groups // chunks
-    for step in range(steps):
-        copies[len(small) + step].wait()
-        x = x_ref[step * block : (step + 1) * block, :]
+
+    def product(step):
+        x = x_ref[step * seqs : (step + 1) * seqs].reshape(seqs * residues, channels)
         centred = x - jnp.mean(x, axis=-1, keepdims=True)
         spread = jnp.mean(jnp.square(centred), axis=-1, keepdims=True)
         p_ref[step] = multiply(centred) * lax.rsqrt(spread + EPS) + offset
+
+    def place(step):
         to = slice(step * seqs, (step + 1) * seqs)
         for g in range(groups):
             rows = [p_ref[step, pl.ds(g * per + e, seqs, stride=residues), :] for e in range(per)]
-            for side in range(2):
+            for side, ref, at in ((0, left_ref, g), (1, right_ref, chunk * groups + g)):
                 value = None
                 for e in range(per):
-                    shift = (e - side) % per * width
-                    placed = pltpu.roll(rows[e], shift, 1) if shift else rows[e]
+                    turn = (e - side) % per * width
+                    placed = pltpu.roll(rows[e], turn, 1) if turn else rows[e]
                     value = placed if value is None else jnp.where(lane == e, placed, value)
-                if side:
-                    right_ref[to, g * LANES : (g + 1) * LANES] = value
-                else:
-                    at = g % share
-                    left_refs[g // share][to, at * LANES : (at + 1) * LANES] = value
-
-
-def project(place, alignment, gain, bias, left_weight, right_weight, chunks):
-    seq_local, residues, channels = alignment.shape
-    width = left_weight.shape[1]
+                ref[to, at * LANES : (at + 1) * LANES] = value
+
+    for step in range(steps):
+        if not chunk:
+            blocks[step].wait()
+        product(step)
+        if step:
+            place(step - 1)
+    place(steps - 1)
+    if not chunk:
+        rest.wait()
+
+
+def project(scalars, alignment, residues, small, given, width):
+    seq_local, left_over, channels = alignment.shape
     steps = 4
-    seqs = seq_local // steps
     span = residues * width
-    outs = [jax.ShapeDtypeStruct((seq_local, span // chunks), F32)] * chunks + [
+    vmem = pl.BlockSpec(memory_space=pltpu.VMEM)
+    smem = pl.BlockSpec(memory_space=pltpu.SMEM)
+    hbm = pl.BlockSpec(memory_space=pltpu.HBM)
+    outs = [
         jax.ShapeDtypeStruct((seq_local, span), F32),
+        jax.ShapeDtypeStruct((seq_local, span * (2 if given else 1)), F32),
     ]
-    return pl.pallas_call(
-        functools.partial(project_kernel, seqs, residues, width, chunks),
+    scratch = [pltpu.VMEM((steps, seq_local // steps * residues, LANES), F32)]
+    if given:
+        arrays = [alignment, *given]
+        specs = [vmem] * len(arrays)
+    else:
+        arrays = [pltpu.with_memory_space_constraint(a, pltpu.HBM) for a in (alignment, *small)]
+        specs = [hbm] * len(arrays)
+        outs += [
+            jax.ShapeDtypeStruct((channels, 2 * LANES), BF16),
+            jax.ShapeDtypeStruct((8, LANES), F32),
+            jax.ShapeDtypeStruct((seq_local, left_over - residues, channels), F32),
+        ]
+        scratch += [
+            pltpu.VMEM((seq_local, residues, channels), F32),
+            pltpu.SemaphoreType.DMA((steps + len(small) + 1,)),
+        ]
+        scratch += [pltpu.VMEM(a.shape, F32) for a in small]
+    return pl.pallas_call(
+        functools.partial(project_kernel, 1 if given else 0, steps, width),
         out_shape=outs,
-        in_specs=[pl.BlockSpec(memory_space=pltpu.SMEM)] * 2 + [pl.BlockSpec(memory_space=pltpu.HBM)] * 5,
-        out_specs=[pl.BlockSpec(memory_space=pltpu.VMEM)] * len(outs),
-        scratch_shapes=[
-            pltpu.VMEM((seq_local * residues, channels), F32),
-            pltpu.VMEM((1, channels), F32),
-            pltpu.VMEM((1, channels), F32),
-            pltpu.VMEM((width, channels), F32),
-            pltpu.VMEM((width, channels), F32),
-            pltpu.SemaphoreType.DMA((4 + steps,)),
-            pltpu.VMEM((channels, 2 * LANES), BF16),
-            pltpu.VMEM((steps, seqs * residues, LANES), F32),
-        ],
-        cost_estimate=pl.CostEstimate(flops=6 * 10**9, bytes_accessed=4 * 10**6, transcendentals=0),
+        in_specs=[smem] * 2 + specs,
+        out_specs=[vmem] * len(outs),
+        scratch_shapes=scratch,
+        cost_estimate=pl.CostEstimate(flops=3 * 10**9, bytes_accessed=2 * 10**6, transcendentals=0),
         compiler_params=pltpu.CompilerParams(vmem_limit_bytes=VMEM),
         name="project",
-    )(
-        *place,
-        *(
-            pltpu.with_memory_space_constraint(a, pltpu.HBM)
-            for a in (
-                alignment.reshape(seq_local * residues, channels),
-                gain.reshape(1, channels),
-                bias.reshape(1, channels),
-                left_weight.T,
-                right_weight.T,
-            )
-        )
-    )
+    )(*scalars, *arrays)
 
 
 def weights_kernel(width, wp_ref, wh_ref, wf_ref, wp_out, wh_out, wf_out):
@@ -354,7 +371,12 @@
     col = lax.axis_index("col")
     shift = jnp.bitwise_xor(lax.div(col, fold), lax.axis_index("row")).astype(jnp.int32).reshape(1)
     member = lax.rem(col, fold).astype(jnp.int32).reshape(1)
-    *lefts, right = project((shift, member), alignment, align_gain, align_bias, left_weight, right_weight, chunks)
+    small = (align_gain.reshape(1, -1), align_bias.reshape(1, -1), left_weight.T, right_weight.T)
+    scalars = (shift, member)
+    part = residues // chunks
+    first, right, *shared, rest = project(scalars, alignment, part, small, (), width)
+    second, right = project(scalars, rest, part, (), (*shared, right), width)
+    lefts = [first, second]
 
     def spread(left):
         return [left] + [along_groups(left, [(a, a ^ m) for a in range(rows)]) for m in range(1, rows)]

time: 66.4 us -> 65.4 us (0.985)
  waiting for transfers between devices: 26.6 us -> 25.5 us
    ppermute x6, waiting for transfers between devices: 16.5 us -> 15.4 us  [along_groups(): lax.ppermute(value, 'col', [(a * fold + k, b * fold + k) for a, b in pair...]
    pallas_call x1 -> x2, Pallas kernels: 3.37 us -> 3.41 us  [project(): pl.pallas_call(functools.partial(project_kernel, 1 if given else 0, steps...]
  transfers between devices with their start and end apart: 17 -> 17, of which waited for: 4 -> 4; matrix products, arithmetic and copies ran while one was open for 0% -> 0% of each run, Pallas kernels for 17% -> 19%
where the time goes in v3:
time: 65.4 us; the launch traced here: 65.3 us
  waiting for transfers between devices  25.5 us (39%)
  starting transfers between devices  21.3 us (33%)
  Pallas kernels  18 us (28%)
    ppermute x6, waiting for transfers between devices, along_groups(): lax.ppermute(value, 'col', [(a * fold + k, b * fold + k) for a, b in pair...  15.4 us
    pallas_call x4, Pallas kernels, pair_update(): pl.pallas_call(functools.partial(pair_kernel, len(lefts), steps, tile, wi...  12.9 us
    ppermute x9, waiting for transfers between devices, along_rows(): return lax.ppermute(value, 'row', [(a, a ^ m) for a in range(rows)])  10.1 us
    ppermute x9, starting transfers between devices, along_rows(): return lax.ppermute(value, 'row', [(a, a ^ m) for a in range(rows)])  8.95 us
    ppermute x6, starting transfers between devices, along_groups(): lax.ppermute(value, 'col', [(a * fold + k, b * fold + k) for a, b in pair...  6.23 us
    ppermute x2, starting transfers between devices, along_members(): return lax.ppermute(value, 'col', [(a, a ^ n) for a in range(cols)])  6.15 us
    pallas_call x2, Pallas kernels, project(): pl.pallas_call(functools.partial(project_kernel, 1 if given else 0, steps...  3.41 us
  transfers between devices with their start and end apart: 17, of which 4 were waited for; matrix products, arithmetic and copies ran while one was open for 0% of the time, Pallas kernels for 19%

profile of v3, /device:TPU:17, one launch (start us, length us, event | category | flops | bytes accessed | tf_op | source)
XLA Modules:
  0.0 65.3 jit_solution(9659138380914088497)
XLA Ops:
  0.0 2.5 %project.2 = (f32[64,512]{1,0:T(8,128)S(1)}, f32[64,512]{1,0:T(8,128)S(1)}, bf16[256,256]{1,0:T(8,128)(2,1)S(1)}, f32[8,128]{1,0:T(8,128)S(1)}, f32[64,16,256]{2,1,0:T(8,128)S(1)}) custom-call(s32[1]{0:T(128)} %bitcast.1.shift_ref.t_ref, s32[1]{0:T(128)} %bitcast.member_ref.at_ref, f32[64,32,256]{2,1,0:T(8,128)} %x_hbm.1, f32[1,256]{1,0:T(1,128)} %bitcast.33, ...), custom_call_target="tpu_custom_call" | custom-call | flops 3000000000 | bytes 2000000 | tf_op jit(solution)/shard_map/project/pallas_call | solution.py:136
  2.5 1.4 %collective-permute-start.10 = (f32[64,512]{1,0:T(8,128)S(1)}, f32[64,512]{1,0:T(8,128)S(1)}, u32[]{:S(2)}, u32[]{:S(2)}) collective-permute-start(f32[64,512]{1,0:T(8,128)S(1)} %get-tuple-element.36.refs_0_), channel_id=1, source_target_pairs={{0,2},{1,3},{2,0},{3,1},{4,6},{5,7},{6,4},{7,5},{8,10},{9,11},{10,... | collective-permute-start | bytes 393224 | tf_op jit(solution)/shard_map/ppermute | solution.py:363
  3.9 0.1 collective-permute-start.11
  3.9 1.3 %collective-permute-start.12 = (f32[64,512]{1,0:T(8,128)S(1)}, f32[64,512]{1,0:T(8,128)S(1)}, u32[]{:S(2)}, u32[]{:S(2)}) collective-permute-start(f32[64,512]{1,0:T(8,128)S(1)} %get-tuple-element.36.refs_0_), channel_id=1, source_target_pairs={{0,6},{1,7},{2,4},{3,5},{4,2},{5,3},{6,0},{7,1},{8,14},{9,15},{10,... | collective-permute-start | bytes 393224 | tf_op jit(solution)/shard_map/ppermute | solution.py:363
  5.2 0.9 %project.3 = (f32[64,512]{1,0:T(8,128)S(1)}, f32[64,1024]{1,0:T(8,128)S(1)}) custom-call(s32[1]{0:T(128)} %bitcast.1.shift_ref.t_ref, s32[1]{0:T(128)} %bitcast.member_ref.at_ref, f32[64,16,256]{2,1,0:T(8,128)S(1)} %get-tuple-element.23.x_hbm, bf16[256,256]{1,0:T(8,128)(2,1)S(1)} %get-tuple-element.24.refs_0_, f32[8,128]{1,0:T(8,128)S(1)} %get-tuple-element.25.refs_1_, ...), custom_call_target="tpu_custom_call" | custom-call | flops 3000000000 | bytes 2000000 | tf_op jit(solution)/shard_map/project/pallas_call | solution.py:136
  6.1 0.0 copy-start.6
  6.2 0.0 copy-start.7
  6.2 0.0 copy-start.8
  6.2 2.3 %collective-permute-start = (f32[64,512]{1,0:T(8,128)S(1)}, f32[64,512]{1,0:T(8,128)S(1)}, u32[]{:S(2)}, u32[]{:S(2)}) collective-permute-start(f32[64,512]{1,0:T(8,128)S(1)} %get-tuple-element.27.refs_0_), channel_id=1, source_target_pairs={{0,2},{1,3},{2,0},{3,1},{4,6},{5,7},{6,4},{7,5},{8,10},{9,11},{10,... | collective-permute-start | bytes 393224 | tf_op jit(solution)/shard_map/ppermute | solution.py:363
  8.4 0.0 collective-permute-start.1
  8.4 0.0 collective-permute-done.10.refs_1_
  8.4 1.3 %collective-permute-start.2 = (f32[64,512]{1,0:T(8,128)S(1)}, f32[64,512]{1,0:T(8,128)S(1)}, u32[]{:S(2)}, u32[]{:S(2)}) collective-permute-start(f32[64,512]{1,0:T(8,128)S(1)} %get-tuple-element.27.refs_0_), channel_id=1, source_target_pairs={{0,6},{1,7},{2,4},{3,5},{4,2},{5,3},{6,0},{7,1},{8,14},{9,15},{10,... | collective-permute-start | bytes 393224 | tf_op jit(solution)/shard_map/ppermute | solution.py:363
  9.7 0.2 collective-permute-done.11.refs_2_
  9.9 12.3 %collective-permute-done.12.refs_3_ = f32[64,512]{1,0:T(8,128)S(1)} collective-permute-done((f32[64,512]{1,0:T(8,128)S(1)}, f32[64,512]{1,0:T(8,128)S(1)}, u32[]{:S(2)}, u32[]{:S(2)}) %collective-permute-start.12) | collective-permute-done | bytes 131104 | tf_op jit(solution)/shard_map/ppermute | solution.py:363
  22.3 1.3 %collective-permute-start.13 = (f32[64,512]{1,0:T(8,128)S(1)}, f32[64,512]{1,0:T(8,128)S(1)}, u32[]{:S(2)}, u32[]{:S(2)}) collective-permute-start(f32[64,512]{1,0:T(8,128)S(1)} %get-tuple-element.38), channel_id=1, source_target_pairs={{0,8},{8,0},{16,24},{24,16},{1,9},{9,1},{17,25},{25,17},{2,10},{10... | collective-permute-start | bytes 393224 | tf_op jit(solution)/shard_map/ppermute | solution.py:366
  23.6 1.3 %collective-permute-start.14 = (f32[64,512]{1,0:T(8,128)S(1)}, f32[64,512]{1,0:T(8,128)S(1)}, u32[]{:S(2)}, u32[]{:S(2)}) collective-permute-start(f32[64,512]{1,0:T(8,128)S(1)} %get-tuple-element.39), channel_id=1, source_target_pairs={{0,16},{8,24},{16,0},{24,8},{1,17},{9,25},{17,1},{25,9},{2,18},{10... | collective-permute-start | bytes 393224 | tf_op jit(solution)/shard_map/ppermute | solution.py:366
  24.8 0.0 collective-permute-done.refs_1_
  24.8 0.2 collective-permute-start.15
  25.0 0.0 collective-permute-done.1.refs_2_
  25.0 2.8 %collective-permute-done.2.refs_3_ = f32[64,512]{1,0:T(8,128)S(1)} collective-permute-done((f32[64,512]{1,0:T(8,128)S(1)}, f32[64,512]{1,0:T(8,128)S(1)}, u32[]{:S(2)}, u32[]{:S(2)}) %collective-permute-start.2) | collective-permute-done | bytes 131104 | tf_op jit(solution)/shard_map/ppermute | solution.py:363
  27.9 0.2 route.2
  28.1 1.3 %collective-permute-start.3 = (f32[64,512]{1,0:T(8,128)S(1)}, f32[64,512]{1,0:T(8,128)S(1)}, u32[]{:S(2)}, u32[]{:S(2)}) collective-permute-start(f32[64,512]{1,0:T(8,128)S(1)} %get-tuple-element.29), channel_id=1, source_target_pairs={{0,8},{8,0},{16,24},{24,16},{1,9},{9,1},{17,25},{25,17},{2,10},{10... | collective-permute-start | bytes 393224 | tf_op jit(solution)/shard_map/ppermute | solution.py:366
  29.4 1.3 %collective-permute-start.4 = (f32[64,512]{1,0:T(8,128)S(1)}, f32[64,512]{1,0:T(8,128)S(1)}, u32[]{:S(2)}, u32[]{:S(2)}) collective-permute-start(f32[64,512]{1,0:T(8,128)S(1)} %get-tuple-element.30), channel_id=1, source_target_pairs={{0,16},{8,24},{16,0},{24,8},{1,17},{9,25},{17,1},{25,9},{2,18},{10... | collective-permute-start | bytes 393224 | tf_op jit(solution)/shard_map/ppermute | solution.py:366
  30.6 0.0 collective-permute-done.13.refs_1_
  30.6 0.3 collective-permute-start.7
  30.9 0.0 collective-permute-done.14.refs_2_
  30.9 0.2 collective-permute-start.8
  31.1 0.0 collective-permute-done.15.refs_3_
  31.1 2.2 %collective-permute-start.9 = (f32[64,1024]{1,0:T(8,128)S(1)}, f32[64,1024]{1,0:T(8,128)S(1)}, u32[]{:S(2)}, u32[]{:S(2)}) collective-permute-start(f32[64,1024]{1,0:T(8,128)S(1)} %get-tuple-element.32.refs_0_), channel_id=1, source_target_pairs={{0,24},{8,16},{16,8},{24,0},{1,25},{9,17},{17,9},{25,1},{2,26},{10... | collective-permute-start | bytes 786440 | tf_op jit(solution)/shard_map/ppermute | solution.py:366
  33.3 0.0 collective-permute-done.3.refs_1_
  33.3 3.9 %collective-permute-start.16 = (f32[256,512]{1,0:T(8,128)S(1)}, f32[256,512]{1,0:T(8,128)S(1)}, u32[]{:S(2)}, u32[]{:S(2)}) collective-permute-start(f32[256,512]{1,0:T(8,128)S(1)} %pack.3.refs_0_), channel_id=1, source_target_pairs={{0,1},{1,0},{2,3},{3,2},{4,5},{5,4},{6,7},{7,6},{8,9},{9,8},{10,11... | collective-permute-start | bytes 1572872 | tf_op jit(solution)/shard_map/ppermute | solution.py:369
  37.2 0.0 collective-permute-done.4.refs_2_
  37.2 1.1 %collective-permute-start.5 = (f32[64,512]{1,0:T(8,128)S(1)}, f32[64,512]{1,0:T(8,128)S(1)}, u32[]{:S(2)}, u32[]{:S(2)}) collective-permute-start(f32[64,512]{1,0:T(8,128)S(1)} %get-tuple-element.31), channel_id=1, source_target_pairs={{0,24},{8,16},{16,8},{24,0},{1,25},{9,17},{17,9},{25,1},{2,26},{10... | collective-permute-start | bytes 393224 | tf_op jit(solution)/shard_map/ppermute | solution.py:366
  38.3 10.1 %collective-permute-done.5.refs_3_ = f32[64,512]{1,0:T(8,128)S(1)} collective-permute-done((f32[64,512]{1,0:T(8,128)S(1)}, f32[64,512]{1,0:T(8,128)S(1)}, u32[]{:S(2)}, u32[]{:S(2)}) %collective-permute-start.5) | collective-permute-done | bytes 131104 | tf_op jit(solution)/shard_map/ppermute | solution.py:366
  48.4 2.3 %collective-permute-start.6 = (f32[256,512]{1,0:T(8,128)S(1)}, f32[256,512]{1,0:T(8,128)S(1)}, u32[]{:S(2)}, u32[]{:S(2)}) collective-permute-start(f32[256,512]{1,0:T(8,128)S(1)} %pack.2.refs_0_), channel_id=1, source_target_pairs={{0,1},{1,0},{2,3},{3,2},{4,5},{5,4},{6,7},{7,6},{8,9},{9,8},{10,11... | collective-permute-start | bytes 1572872 | tf_op jit(solution)/shard_map/ppermute | solution.py:369
  50.7 0.0 copy-done.6
  50.7 0.0 copy-done.7
  50.7 0.0 copy-done.8
  50.7 0.4 weights.1
  51.1 0.0 copy-start
  51.2 0.0 copy-start.1
  51.2 0.0 copy-start.2
  51.2 0.0 copy-start.3
  51.2 0.0 copy-start.4
  51.2 0.0 copy-start.5
  51.2 0.0 collective-permute-done.7.refs_1_
  51.2 0.0 collective-permute-done.8.refs_2_
  51.2 0.0 collective-permute-done.9.refs_3_
  51.3 1.0 %turn.1.refs_1_ = bf16[1024,768]{1,0:T(8,128)(2,1)S(1)} custom-call(f32[64,1024]{1,0:T(8,128)S(1)} %get-tuple-element.32.refs_0_, f32[64,1024]{1,0:T(8,128)S(1)} %collective-permute-done.7.refs_1_, f32[64,1024]{1,0:T(8,128)S(1)} %collective-permute-done.8.refs_2_, f32[64,1024]{1,0:T(8,128)S(1)} %collective-permute-done.9.refs_3_), custom_call_target="tpu_custom_call" | custom-call | flops 2000000000 | bytes 3000000 | tf_op jit(solution)/shard_map/turn/pallas_call | solution.py:197
  52.2 0.2 copy-done
  52.4 0.0 copy-done.1
  52.4 0.0 copy-done.2
  52.4 0.0 copy-done.3
  52.4 0.0 copy-done.4
  52.4 0.0 copy-done.5
  52.4 3.2 %pair.4.refs_11_ = f32[64,32,128]{2,1,0:T(8,128)} custom-call(s32[1]{0:T(128)} %bitcast.member_ref.at_ref, f32[256,512]{1,0:T(8,128)S(1)} %pack.3.refs_0_, bf16[1024,768]{1,0:T(8,128)(2,1)S(1)} %turn.1.refs_1_, bf16[1024,256]{1,0:T(8,128)(2,1)S(1)} %get-tuple-element.33.refs_2_, bf16[384,512]{1,0:T(8,128)(2,1)S(1)} %get-tuple-element.34.refs_3_, ...), custom_call_target="tpu_custom_call" | custom-call | flops 1000000000 | bytes 4000000 | tf_op jit(solution)/shard_map/pair/pallas_call | solution.py:319
  55.6 0.0 collective-permute-done.16.refs_0_
  55.6 3.2 %pair.5.refs_11_ = f32[64,32,128]{2,1,0:T(8,128)} custom-call(s32[1]{0:T(128)} %bitcast.member_ref.at_ref, f32[256,512]{1,0:T(8,128)S(1)} %collective-permute-done.16.refs_0_, bf16[1024,768]{1,0:T(8,128)(2,1)S(1)} %turn.1.refs_1_, bf16[1024,256]{1,0:T(8,128)(2,1)S(1)} %get-tuple-element.33.refs_2_, ...), custom_call_target="tpu_custom_call", output_to_operand_aliasing={{}: (12, {})} | custom-call | flops 1000000000 | bytes 4000000 | tf_op jit(solution)/shard_map/pair/pallas_call | solution.py:319
  58.8 3.2 %pair.6.refs_11_ = f32[64,32,128]{2,1,0:T(8,128)} custom-call(s32[1]{0:T(128)} %bitcast.member_ref.at_ref, f32[256,512]{1,0:T(8,128)S(1)} %pack.2.refs_0_, bf16[1024,768]{1,0:T(8,128)(2,1)S(1)} %turn.1.refs_1_, bf16[1024,256]{1,0:T(8,128)(2,1)S(1)} %get-tuple-element.33.refs_2_, ...), custom_call_target="tpu_custom_call", output_to_operand_aliasing={{}: (12, {})} | custom-call | flops 1000000000 | bytes 4000000 | tf_op jit(solution)/shard_map/pair/pallas_call | solution.py:319
  62.1 0.0 collective-permute-done.6.refs_0_
  62.1 3.2 %pair.7 = f32[64,32,128]{2,1,0:T(8,128)} custom-call(s32[1]{0:T(128)} %bitcast.member_ref.at_ref, f32[256,512]{1,0:T(8,128)S(1)} %collective-permute-done.6.refs_0_, bf16[1024,768]{1,0:T(8,128)(2,1)S(1)} %turn.1.refs_1_, bf16[1024,256]{1,0:T(8,128)(2,1)S(1)} %get-tuple-element.33.refs_2_, ...), custom_call_target="tpu_custom_call", output_to_operand_aliasing={{}: (12, {})} | custom-call | flops 1000000000 | bytes 4000000 | tf_op jit(solution)/shard_map/pair/pallas_call | solution.py:319
  (3 shorter events, 0.1 us)
Async XLA Ops:
  2.5 5.9 %collective-permute-start.10 = (f32[64,512]{1,0:T(8,128)S(1)}, f32[64,512]{1,0:T(8,128)S(1)}, u32[]{:S(2)}, u32[]{:S(2)}) collective-permute-start(f32[64,512]{1,0:T(8,128)S(1)} %get-tuple-element.36.refs_0_), channel_id=1, source_target_pairs={{0,2},{1,3},{2,0},{3,1},{4,6},{5,7},{6,4},{7,5},{8,10},{9,11},{10,... | collective-permute-start | bytes 393224 | tf_op jit(solution)/shard_map/ppermute | solution.py:363
  3.9 6.0 %collective-permute-start.11 = (f32[64,512]{1,0:T(8,128)S(1)}, f32[64,512]{1,0:T(8,128)S(1)}, u32[]{:S(2)}, u32[]{:S(2)}) collective-permute-start(f32[64,512]{1,0:T(8,128)S(1)} %get-tuple-element.36.refs_0_), channel_id=1, source_target_pairs={{0,4},{1,5},{2,6},{3,7},{4,0},{5,1},{6,2},{7,3},{8,12},{9,13},{10,... | collective-permute-start | bytes 393224 | tf_op jit(solution)/shard_map/ppermute | solution.py:363
  3.9 18.3 %collective-permute-start.12 = (f32[64,512]{1,0:T(8,128)S(1)}, f32[64,512]{1,0:T(8,128)S(1)}, u32[]{:S(2)}, u32[]{:S(2)}) collective-permute-start(f32[64,512]{1,0:T(8,128)S(1)} %get-tuple-element.36.refs_0_), channel_id=1, source_target_pairs={{0,6},{1,7},{2,4},{3,5},{4,2},{5,3},{6,0},{7,1},{8,14},{9,15},{10,... | collective-permute-start | bytes 393224 | tf_op jit(solution)/shard_map/ppermute | solution.py:363
  6.1 44.6 %copy-start.6 = (f32[1024,128]{1,0:T(8,128)S(1)}, f32[1024,128]{1,0:T(8,128)}, u32[]{:S(2)}) copy-start(f32[1024,128]{1,0:T(8,128)} %wp_ref.1) | copy-start | bytes 1572868
  6.2 44.5 %copy-start.7 = (f32[128,512]{1,0:T(8,128)S(1)}, f32[128,512]{1,0:T(8,128)}, u32[]{:S(2)}) copy-start(f32[128,512]{1,0:T(8,128)} %wh_ref.1) | copy-start | bytes 786436
  6.2 44.5 %copy-start.8 = (f32[512,128]{1,0:T(8,128)S(1)}, f32[512,128]{1,0:T(8,128)}, u32[]{:S(2)}) copy-start(f32[512,128]{1,0:T(8,128)} %wf_ref.1) | copy-start | bytes 786436
  6.2 18.7 %collective-permute-start = (f32[64,512]{1,0:T(8,128)S(1)}, f32[64,512]{1,0:T(8,128)S(1)}, u32[]{:S(2)}, u32[]{:S(2)}) collective-permute-start(f32[64,512]{1,0:T(8,128)S(1)} %get-tuple-element.27.refs_0_), channel_id=1, source_target_pairs={{0,2},{1,3},{2,0},{3,1},{4,6},{5,7},{6,4},{7,5},{8,10},{9,11},{10,... | collective-permute-start | bytes 393224 | tf_op jit(solution)/shard_map/ppermute | solution.py:363
  8.4 16.6 %collective-permute-start.1 = (f32[64,512]{1,0:T(8,128)S(1)}, f32[64,512]{1,0:T(8,128)S(1)}, u32[]{:S(2)}, u32[]{:S(2)}) collective-permute-start(f32[64,512]{1,0:T(8,128)S(1)} %get-tuple-element.27.refs_0_), channel_id=1, source_target_pairs={{0,4},{1,5},{2,6},{3,7},{4,0},{5,1},{6,2},{7,3},{8,12},{9,13},{10,... | collective-permute-start | bytes 393224 | tf_op jit(solution)/shard_map/ppermute | solution.py:363
  8.4 19.4 %collective-permute-start.2 = (f32[64,512]{1,0:T(8,128)S(1)}, f32[64,512]{1,0:T(8,128)S(1)}, u32[]{:S(2)}, u32[]{:S(2)}) collective-permute-start(f32[64,512]{1,0:T(8,128)S(1)} %get-tuple-element.27.refs_0_), channel_id=1, source_target_pairs={{0,6},{1,7},{2,4},{3,5},{4,2},{5,3},{6,0},{7,1},{8,14},{9,15},{10,... | collective-permute-start | bytes 393224 | tf_op jit(solution)/shard_map/ppermute | solution.py:363
  22.3 8.3 %collective-permute-start.13 = (f32[64,512]{1,0:T(8,128)S(1)}, f32[64,512]{1,0:T(8,128)S(1)}, u32[]{:S(2)}, u32[]{:S(2)}) collective-permute-start(f32[64,512]{1,0:T(8,128)S(1)} %get-tuple-element.38), channel_id=1, source_target_pairs={{0,8},{8,0},{16,24},{24,16},{1,9},{9,1},{17,25},{25,17},{2,10},{10... | collective-permute-start | bytes 393224 | tf_op jit(solution)/shard_map/ppermute | solution.py:366
  23.6 7.3 %collective-permute-start.14 = (f32[64,512]{1,0:T(8,128)S(1)}, f32[64,512]{1,0:T(8,128)S(1)}, u32[]{:S(2)}, u32[]{:S(2)}) collective-permute-start(f32[64,512]{1,0:T(8,128)S(1)} %get-tuple-element.39), channel_id=1, source_target_pairs={{0,16},{8,24},{16,0},{24,8},{1,17},{9,25},{17,1},{25,9},{2,18},{10... | collective-permute-start | bytes 393224 | tf_op jit(solution)/shard_map/ppermute | solution.py:366
  24.8 6.3 %collective-permute-start.15 = (f32[64,512]{1,0:T(8,128)S(1)}, f32[64,512]{1,0:T(8,128)S(1)}, u32[]{:S(2)}, u32[]{:S(2)}) collective-permute-start(f32[64,512]{1,0:T(8,128)S(1)} %get-tuple-element.40), channel_id=1, source_target_pairs={{0,24},{8,16},{16,8},{24,0},{1,25},{9,17},{17,9},{25,1},{2,26},{10... | collective-permute-start | bytes 393224 | tf_op jit(solution)/shard_map/ppermute | solution.py:366
  28.1 5.2 %collective-permute-start.3 = (f32[64,512]{1,0:T(8,128)S(1)}, f32[64,512]{1,0:T(8,128)S(1)}, u32[]{:S(2)}, u32[]{:S(2)}) collective-permute-start(f32[64,512]{1,0:T(8,128)S(1)} %get-tuple-element.29), channel_id=1, source_target_pairs={{0,8},{8,0},{16,24},{24,16},{1,9},{9,1},{17,25},{25,17},{2,10},{10... | collective-permute-start | bytes 393224 | tf_op jit(solution)/shard_map/ppermute | solution.py:366
  29.4 7.8 %collective-permute-start.4 = (f32[64,512]{1,0:T(8,128)S(1)}, f32[64,512]{1,0:T(8,128)S(1)}, u32[]{:S(2)}, u32[]{:S(2)}) collective-permute-start(f32[64,512]{1,0:T(8,128)S(1)} %get-tuple-element.30), channel_id=1, source_target_pairs={{0,16},{8,24},{16,0},{24,8},{1,17},{9,25},{17,1},{25,9},{2,18},{10... | collective-permute-start | bytes 393224 | tf_op jit(solution)/shard_map/ppermute | solution.py:366
  30.6 20.6 %collective-permute-start.7 = (f32[64,1024]{1,0:T(8,128)S(1)}, f32[64,1024]{1,0:T(8,128)S(1)}, u32[]{:S(2)}, u32[]{:S(2)}) collective-permute-start(f32[64,1024]{1,0:T(8,128)S(1)} %get-tuple-element.32.refs_0_), channel_id=1, source_target_pairs={{0,8},{8,0},{16,24},{24,16},{1,9},{9,1},{17,25},{25,17},{2,10},{10... | collective-permute-start | bytes 786440 | tf_op jit(solution)/shard_map/ppermute | solution.py:366
  30.9 20.3 %collective-permute-start.8 = (f32[64,1024]{1,0:T(8,128)S(1)}, f32[64,1024]{1,0:T(8,128)S(1)}, u32[]{:S(2)}, u32[]{:S(2)}) collective-permute-start(f32[64,1024]{1,0:T(8,128)S(1)} %get-tuple-element.32.refs_0_), channel_id=1, source_target_pairs={{0,16},{8,24},{16,0},{24,8},{1,17},{9,25},{17,1},{25,9},{2,18},{10... | collective-permute-start | bytes 786440 | tf_op jit(solution)/shard_map/ppermute | solution.py:366
  31.1 20.1 %collective-permute-start.9 = (f32[64,1024]{1,0:T(8,128)S(1)}, f32[64,1024]{1,0:T(8,128)S(1)}, u32[]{:S(2)}, u32[]{:S(2)}) collective-permute-start(f32[64,1024]{1,0:T(8,128)S(1)} %get-tuple-element.32.refs_0_), channel_id=1, source_target_pairs={{0,24},{8,16},{16,8},{24,0},{1,25},{9,17},{17,9},{25,1},{2,26},{10... | collective-permute-start | bytes 786440 | tf_op jit(solution)/shard_map/ppermute | solution.py:366
  33.3 22.3 %collective-permute-start.16 = (f32[256,512]{1,0:T(8,128)S(1)}, f32[256,512]{1,0:T(8,128)S(1)}, u32[]{:S(2)}, u32[]{:S(2)}) collective-permute-start(f32[256,512]{1,0:T(8,128)S(1)} %pack.3.refs_0_), channel_id=1, source_target_pairs={{0,1},{1,0},{2,3},{3,2},{4,5},{5,4},{6,7},{7,6},{8,9},{9,8},{10,11... | collective-permute-start | bytes 1572872 | tf_op jit(solution)/shard_map/ppermute | solution.py:369
  37.2 11.2 %collective-permute-start.5 = (f32[64,512]{1,0:T(8,128)S(1)}, f32[64,512]{1,0:T(8,128)S(1)}, u32[]{:S(2)}, u32[]{:S(2)}) collective-permute-start(f32[64,512]{1,0:T(8,128)S(1)} %get-tuple-element.31), channel_id=1, source_target_pairs={{0,24},{8,16},{16,8},{24,0},{1,25},{9,17},{17,9},{25,1},{2,26},{10... | collective-permute-start | bytes 393224 | tf_op jit(solution)/shard_map/ppermute | solution.py:366
  48.4 13.7 %collective-permute-start.6 = (f32[256,512]{1,0:T(8,128)S(1)}, f32[256,512]{1,0:T(8,128)S(1)}, u32[]{:S(2)}, u32[]{:S(2)}) collective-permute-start(f32[256,512]{1,0:T(8,128)S(1)} %pack.2.refs_0_), channel_id=1, source_target_pairs={{0,1},{1,0},{2,3},{3,2},{4,5},{5,4},{6,7},{7,6},{8,9},{9,8},{10,11... | collective-permute-start | bytes 1572872 | tf_op jit(solution)/shard_map/ppermute | solution.py:369
  51.1 1.2 %copy-start = (f32[64,32,128]{2,1,0:T(8,128)S(1)}, f32[64,32,128]{2,1,0:T(8,128)}, u32[]{:S(2)}) copy-start(f32[64,32,128]{2,1,0:T(8,128)} %refs_10_.7) | copy-start | bytes 3145732
  51.2 1.2 %copy-start.1 = (f32[512]{0:T(512)S(1)}, f32[512]{0:T(512)}, u32[]{:S(2)}) copy-start(f32[512]{0:T(512)} %param.25) | copy-start | bytes 6148
  51.2 1.2 %copy-start.2 = (f32[128]{0:T(128)S(1)}, f32[128]{0:T(128)}, u32[]{:S(2)}) copy-start(f32[128]{0:T(128)} %param.20) | copy-start | bytes 1540
  51.2 1.2 %copy-start.3 = (f32[128]{0:T(128)S(1)}, f32[128]{0:T(128)}, u32[]{:S(2)}) copy-start(f32[128]{0:T(128)} %param.22) | copy-start | bytes 1540
  51.2 1.2 %copy-start.4 = (f32[128]{0:T(128)S(1)}, f32[128]{0:T(128)}, u32[]{:S(2)}) copy-start(f32[128]{0:T(128)} %param.23) | copy-start | bytes 1540
  51.2 1.2 %copy-start.5 = (f32[128]{0:T(128)S(1)}, f32[128]{0:T(128)}, u32[]{:S(2)}) copy-start(f32[128]{0:T(128)} %param.27) | copy-start | bytes 1540
